TPU v7x, 32 devices: a whole 2x2x4 slice. The times are simulated.
32 devices in a mesh: site: 8 (over z, x), band: 4 (over y, core).
Axes of the slice: x: 2, y: 2, z: 4, core: 2. Of those that a mesh axis runs over, the one named last changes fastest.
Arguments:
- fields: bfloat16 [1024, 8, 4096], P('site', None, 'band'), may hold values from -6 to 6
- factor: bfloat16 [1024, 4, 128], P('site'), may hold values from -0.25 to 0.25
- pattern: int32 [8, 3], P('site'), may hold values 0 or 1
- tx_power: float32 [1024], replicated, may hold values from 30 to 49
- site_position: float32 [2, 1024], replicated, may hold values from 0 to 1, as said below
- candidates: int32 [8, 16], P('site'), may hold values from 0 to 1023, as said below
Outputs:
- best_level: float32 [8, 4096], P('site', 'band')
- sinr_level: float32 [8, 4096], P('site', 'band')
- tile_mean: float32 [8], P('site')
Inputs may be any that keep to these rules, and one draw needn't show every extreme that they name: `site_position`: tile t covers column t % 8 and row t // 8 of a grid of 8 x (1) tiles over the window. Site s lies in tile s // 128, which is cut into 16 columns by 8 rows of equal cells, each holding exactly one of the tile's sites. The candidates of tile t are its 16 sites in the top row of cells, in order of cell column; they are distinct.
All inputs are finite; a program needn't handle non-finite values. No bound on the sum of `pattern` on one device may be relied on, other than what follows from the above.
Results may differ from a plain program's by a relative error of at most 0.005.
Values may be sent and summed in bfloat16 or wider, within the bound.
No kernel may reach another device: no remote copies, remote signals or barrier semaphores. Data moves between devices by JAX's collectives and lax.ppermute only.
A program may use at most 192 MiB of HBM per device.

v0:
```python
import functools
import math

import jax
import jax.numpy as jnp
from jax import lax
from jax.experimental import pallas as pl
from jax.experimental.pallas import tpu as pltpu
from jax.sharding import PartitionSpec as P


COLS = 256
spacing = 0.03
ln_tenth = 0.2302585093
to_exp2 = ln_tenth * math.log2(math.e)
dist_gain = to_exp2 * 11.0 * math.log10(2.0)
mixed_gain = to_exp2 * 8.0
F32 = jnp.float32
BF16 = jnp.bfloat16
SPARE = 256 << 10
SHARES = 2
HBM = pl.BlockSpec(memory_space=pltpu.HBM)
SMEM = pl.BlockSpec(memory_space=pltpu.SMEM)
VMEM = pl.BlockSpec(memory_space=pltpu.VMEM)


def places():
    return lax.axis_index("site"), lax.axis_index("band")


def grant(*parts):
    size = sum(math.prod(shape) * jnp.dtype(kind).itemsize for shape, kind in parts)
    return pltpu.CompilerParams(vmem_limit_bytes=min(size + (8 << 20), 60 << 20))


def room_for(*parts):
    size = sum(math.prod(shape) * jnp.dtype(kind).itemsize for shape, kind in parts)
    return pltpu.CompilerParams(vmem_limit_bytes=(64 << 20) - size - SPARE)


def split_tiles(fields, factor, pattern, lines):
    block, tiles, pixels = fields.shape
    depth = factor.shape[1]
    chunk = min(block, max(1, 256 // tiles))
    part = block // SHARES
    wide = depth * block
    np_ = 2 * lines

    def kernel(pattern_ref, x_ref, factor_ref, *refs):
        pairs, (coef_out, x_in, factor_in, sems) = refs[:np_], refs[np_:]
        me, band = places()
        copies = [pltpu.make_async_copy(factor_ref.at[pl.ds(band % SHARES * part, part)], factor_in, sems.at[block // chunk])]
        for i in range(block // chunk):
            span = slice(i * chunk, (i + 1) * chunk)
            copies.append(pltpu.make_async_copy(x_ref.at[span], x_in.at[span], sems.at[i]))
        for copy in copies:
            copy.start()
        size = chunk * tiles
        row = lax.broadcasted_iota(jnp.int32, (size, size), 0)
        col = lax.broadcasted_iota(jnp.int32, (size, size), 1)
        slot = row // chunk
        kind, k, j = slot // (2 * lines), slot // 2 % lines, slot % 2
        tile = (2 * (((me // lines) & 1) ^ 1 ^ kind) + j) * lines + ((me % lines) ^ k)
        move = jnp.where(col == row % chunk * tiles + tile, 1.0, 0.0)
        for i in range(block // chunk):
            copies[i + 1].wait()
            for c in range(0, pixels, 256):
                span = slice(c, c + 256)
                x = x_in[i * chunk : (i + 1) * chunk, :, span].astype(F32).reshape(size, 256)
                moved = jnp.dot(move, x, preferred_element_type=F32).astype(BF16)
                for p, pair in enumerate(pairs):
                    for j in range(2):
                        at = (2 * p + j) * chunk
                        pair[j, i * chunk : (i + 1) * chunk, span] = moved[at : at + chunk]
        copies[0].wait()
        row = lax.broadcasted_iota(jnp.int32, (part, block), 0) + band % SHARES * part
        col = lax.broadcasted_iota(jnp.int32, (part, block), 1)
        rows = factor_in[...].astype(F32)
        for d in range(depth):
            keep = col <= row if d == 0 else jnp.full((part, block), pattern_ref[0, d - 1], jnp.int32) != 0
            lane = (depth - 1 - d) * block
            coef_out[:, lane : lane + block] = jnp.where(keep, rows[:, d, :], 0.0).astype(BF16)

    shapes = [((2, block, pixels), BF16)] * np_ + [((part, wide), BF16)]
    scratch = [((block, tiles, pixels), BF16), ((part, depth, block), BF16)]
    out = pl.pallas_call(
        kernel,
        in_specs=[SMEM, HBM, HBM],
        out_specs=[VMEM] * (np_ + 1),
        out_shape=[jax.ShapeDtypeStruct(*shape) for shape in shapes],
        scratch_shapes=[pltpu.VMEM(*one) for one in scratch] + [pltpu.SemaphoreType.DMA((block // chunk + 1,))],
        compiler_params=room_for(*shapes),
        name="split_tiles",
    )(pattern, fields, factor)
    return out[:lines], out[lines:-1], out[-1]


def tile_of(me, lines, j):
    return (2 * (((me // lines) & 1) ^ 1) + j) * lines + me % lines


def column(ref, row, i, block):
    line = ref[pl.ds(row, 1), pl.ds(pl.multiple_of(i * block, block), block)]
    return jnp.broadcast_to(line, (block, block)).T


def geometry(tx_ref, pos_ref, i, block, height):
    xs = column(pos_ref, 0, i, block) * (8.0 * COLS * spacing)
    ys = column(pos_ref, 1, i, block) * (height * COLS * spacing)
    base = to_exp2 * (column(tx_ref, 0, i, block) - 10.0)
    wide = COLS // block
    return jnp.concatenate([xs] * wide, axis=1), ys, jnp.concatenate([base] * wide, axis=1)


def across(xs, tile):
    col = lax.broadcasted_iota(jnp.int32, (1, COLS), 1)
    dx = xs - (tile % 8 * COLS + col).astype(F32) * spacing
    return dx * dx


def reach(dx2, ys, base, tile, row):
    at = jnp.full(ys.shape, tile // 8 * COLS + row, jnp.int32).astype(F32) * spacing
    dy = ys - at
    dy2 = dy * dy + spacing * spacing
    d2 = dx2 + jnp.concatenate([dy2] * (COLS // ys.shape[1]), axis=1)
    return base - dist_gain * jnp.log2(d2)


def rounded(mixed):
    return mixed_gain * mixed.astype(BF16).astype(F32)


def fold(power):
    return jnp.sum(power.reshape(power.shape[0] // 8, 8, power.shape[1]), axis=0)


def pick(cand_ref, j, first_site, pw, top, block):
    pixels = pw.shape[1]
    best = jnp.full((1, pixels), -1.0, F32)
    serving = jnp.zeros((1, pixels), jnp.int32)
    for c in range(cand_ref.shape[1]):
        local = jnp.clip(cand_ref[j, c] - first_site, 0, block - 1)
        power = pw[pl.ds(top + local, 1), :]
        more = power > best
        best = jnp.where(more, power, best)
        serving = jnp.where(more, local, serving)
    rest = []
    for c in range(0, pixels, COLS):
        ids = lax.broadcasted_iota(jnp.int32, (block, COLS), 0)
        mine = pw[pl.ds(top, block), c : c + COLS]
        rest.append(fold(jnp.where(ids == serving[:, c : c + COLS], 0.0, mine)))
    return best, jnp.concatenate(rest, axis=1)


def reach_tables(tx, pos, unit, half, depth, pixels, height):
    n, lines, lead = 2 * half, half // 2, depth - 1
    block = tx.shape[1] // n
    rows = pixels // COLS
    tall = lead * block

    def kernel(tx_ref, pos_ref, unit_ref, table, median, unit_out):
        unit_out[...] = unit_ref[...]
        me, band = places()
        upper = me // half
        low = upper * half
        level = me // lines

        def fill(out, place, i):
            xs, ys, base = geometry(tx_ref, pos_ref, i, block, height)
            for j in range(2):
                tile = tile_of(me, lines, j)
                dx2 = across(xs, tile)
                for r in range(rows):
                    span = slice(r * COLS, (r + 1) * COLS)
                    out[j, pl.ds(place, block), span] = reach(dx2, ys, base, tile, band * rows + r)

        def body(l, carry):
            fill(table, pl.multiple_of(l * block, block), low + l)
            return carry

        lax.fori_loop(upper * lead, half, body, 0)

        @pl.when((level == 1) | (level == 2))
        def _():
            def inner(l, carry):
                fill(median, pl.multiple_of(l * block, block), half + l)
                return carry

            lax.fori_loop(0, lead, inner, 0)

    outs = [((2, half * block, pixels), F32), ((2, tall, pixels), F32), (unit.shape, BF16)]
    flops = 20 * 2 * (half + lead) * block * pixels
    return pl.pallas_call(
        kernel,
        in_specs=[VMEM] * 3,
        out_specs=[VMEM] * 3,
        out_shape=[jax.ShapeDtypeStruct(*out) for out in outs],
        compiler_params=grant(*outs, outs[2]),
        cost_estimate=pl.CostEstimate(flops=flops, bytes_accessed=8 << 20, transcendentals=0),
        name="reach_tables",
    )(tx, pos, unit)


def stage_one(cand, table, pieces, held, partner, half, depth):
    _, block, pixels = held[0].shape
    lead, lines = depth - 1, half // 2
    rows = pixels // COLS
    n, part, wide = 2 * half, pieces[0].shape[3], depth * block
    np_, nh = len(pieces), len(held)
    tall = lead * block

    def kernel(cand_ref, table_ref, *refs):
        piece_refs, refs = refs[:np_], refs[np_:]
        held_refs, refs = refs[:nh], refs[nh:]
        partner_refs, refs = refs[:nh], refs[nh:]
        sums, best_out, partial, coef_cross = refs[:4]
        near, coef, coef_own, group, pw, acc = refs[4:]
        me, band = places()
        upper = me // half
        low = upper * half
        level = me // lines
        inner = (level == 1) | (level == 2)
        views = [piece.at[m] for piece in piece_refs for m in range(piece.shape[0])]
        for m, view in enumerate(views):
            start = pl.multiple_of((band % SHARES ^ m) * part, part)
            for e in range(n):
                coef[me ^ e, pl.ds(start, part), :] = view[e // lines, e % lines]
        near[:, :lead] = jnp.zeros((2, lead, block, pixels), BF16)
        for k in range(lines):
            for j in range(2):
                near[j, lead + (me ^ k) - low] = held_refs[k][j]
                near[j, lead + (me ^ k ^ lines) - low] = partner_refs[k][j]
        acc[...] = jnp.zeros_like(acc)
        best_out[...] = jnp.zeros_like(best_out)

        @pl.when(inner)
        def _():
            up = jnp.full((block, block), upper, jnp.int32) != 0
            for l in range(lead):
                for c in range(lead):
                    zero = jnp.zeros((block, block), BF16)
                    early = coef[half + l, :, (c - l) * block : (c - l + 1) * block] if c >= l else zero
                    at = lead - l + c
                    late = coef[half + l, :, at * block : (at + 1) * block] if c <= l else zero
                    there = (slice(l * block, (l + 1) * block), slice(c * block, (c + 1) * block))
                    early, late = early.astype(F32), late.astype(F32)
                    coef_own[there] = jnp.where(up, late, early).astype(BF16)
                    coef_cross[there] = jnp.where(up, early, late).astype(BF16)
            top = jnp.where(upper == 0, half, lead)
            for j in range(2):
                for r in range(rows):
                    span = slice(r * COLS, (r + 1) * COLS)
                    some = near[j, pl.ds(top, lead), :, span].reshape(tall, COLS)
                    partial[j, :, span] = jnp.dot(coef_own[...], some, preferred_element_type=F32)

        first = upper * lead

        def add(j, i, span, power):
            own = i == tile_of(me, lines, j)

            @pl.when(own)
            def _():
                pw[j, :, span] = power

            acc[j, :, span] += jnp.where(own, 0.0, fold(power))

        @pl.when(upper == 0)
        def _():
            for g in range(0, half, depth):
                count = min(depth, half - g)
                start = max(0, g - lead)
                deep = g + count - start
                for a in range(count):
                    for b in range(deep):
                        d = g + a - start - b
                        there = (slice(a * block, (a + 1) * block), slice(b * block, (b + 1) * block))
                        if 0 <= d < depth:
                            group[there] = coef[g + a, :, (lead - d) * block : (depth - d) * block]
                        else:
                            group[there] = jnp.zeros((block, block), BF16)
                for j in range(2):
                    for r in range(rows):
                        span = slice(r * COLS, (r + 1) * COLS)
                        some = near[j, lead + start : lead + start + deep, :, span].reshape(deep * block, COLS)
                        here = slice(g * block, (g + count) * block)
                        mixed = jnp.dot(group[: count * block, : deep * block], some, preferred_element_type=F32)
                        power = jnp.exp2(table_ref[j, here, span] + rounded(mixed))
                        for a in range(count):
                            add(j, g + a, span, power[a * block : (a + 1) * block])

        @pl.when(upper != 0)
        def _():
            def body(l, carry):
                for j in range(2):
                    for r in range(rows):
                        span = slice(r * COLS, (r + 1) * COLS)
                        some = near[j, pl.ds(l, depth), :, span].reshape(depth * block, COLS)
                        mixed = rounded(jnp.dot(coef[half + l], some, preferred_element_type=F32))
                        here = pl.ds(pl.multiple_of(l * block, block), block)
                        add(j, half + l, span, jnp.exp2(table_ref[j, here, span] + mixed))
                return carry

            lax.fori_loop(lead, half, body, 0)

        for j in range(2):
            tile = tile_of(me, lines, j)

            @pl.when((tile >= low + first) & (tile < low + half))
            def _():
                best, rest = pick(cand_ref, j, tile * block, pw.at[j], 0, block)
                best_out[j : j + 1] = best
                acc[j] += rest

            sums[j : j + 1] = jnp.sum(acc[j], axis=0, keepdims=True)

    flops = (half * 2 + lead) * 2 * block * depth * block * pixels
    scratch = [
        ((2, lead + half, block, pixels), BF16),
        ((n, block, wide), BF16),
        ((tall, tall), BF16),
        ((depth * block, (depth + lead) * block), BF16),
        ((2, block, pixels), F32),
        ((2, 8, pixels), F32),
    ]
    outs = [((2, pixels), F32)] * 2 + [((2, tall, pixels), F32), ((tall, tall), BF16)]
    given = (table, *pieces, *held, *partner)
    return pl.pallas_call(
        kernel,
        in_specs=[SMEM] + [VMEM] * len(given),
        out_specs=[VMEM] * 4,
        out_shape=[jax.ShapeDtypeStruct(*out) for out in outs],
        scratch_shapes=[pltpu.VMEM(*one) for one in scratch],
        compiler_params=grant(*scratch, *outs, *[(x.shape, x.dtype) for x in given]),
        cost_estimate=pl.CostEstimate(flops=flops, bytes_accessed=8 << 20, transcendentals=0),
        name="stage_one",
    )(cand, *given)


def stage_two(cand, one, median, units, half, depth):
    _, block, pixels = units[0][1].shape
    lead, lines = depth - 1, half // 2
    rows = pixels // COLS
    nu = len(units)
    tall = lead * block

    def kernel(cand_ref, sums, best_one, partial, coef, median, *refs):
        unit_refs, refs = refs[:nu], refs[nu:]
        own_out, hop_out, far, pw, acc, best = refs
        me, _ = places()
        upper = me // half
        level = me // lines

        @pl.when((level == 1) | (level == 2))
        def _():
            for (e, _), ref in zip(units, unit_refs):
                place = (me ^ e) - jnp.where(upper == 0, half, half - lead)
                place = jnp.where((place >= 0) & (place < lead), place, lead)
                for j in range(2):
                    far[j, place] = ref[j]
            best[...] = best_one[...]
            for j in range(2):
                tile = tile_of(me, lines, j)
                for r in range(rows):
                    span = slice(r * COLS, (r + 1) * COLS)
                    some = far[j, :lead, :, span].reshape(tall, COLS)
                    mixed = jnp.dot(coef[...], some, preferred_element_type=F32) + partial[j, :, span]
                    power = jnp.exp2(median[j, :, span] + rounded(mixed))
                    total = jnp.zeros((8, COLS), F32)
                    for l in range(lead):
                        total += jnp.where(tile == half + l, 0.0, fold(power[l * block : (l + 1) * block]))
                    acc[:, span] = total

                    @pl.when(upper != 0)
                    def _():
                        pw[:, span] = power

                @pl.when((tile >= half) & (tile < half + lead))
                def _():
                    top = pl.multiple_of((tile - half) * block, block)
                    first, rest = pick(cand_ref, j, tile * block, pw, top, block)
                    best[j : j + 1] = first
                    acc[...] += rest

                total = sums[j : j + 1] + jnp.sum(acc[...], axis=0, keepdims=True)
                mine = (level == 1) == (j == 1)

                def put(out):
                    out[0:1] = best[j : j + 1]
                    out[1:2] = total

                pl.when(mine)(functools.partial(put, own_out))
                pl.when(jnp.logical_not(mine))(functools.partial(put, hop_out))

    scratch = [((2, lead + 1, block, pixels), BF16), ((tall, pixels), F32), ((8, pixels), F32), ((2, pixels), F32)]
    outs = [jax.ShapeDtypeStruct((2, pixels), F32)] * 2
    given = [x for _, x in units]
    held = [(x.shape, x.dtype) for x in (*one[2:], median, *given)]
    return pl.pallas_call(
        kernel,
        in_specs=[SMEM] + [VMEM] * (5 + nu),
        out_specs=[VMEM] * 2,
        out_shape=outs,
        scratch_shapes=[pltpu.VMEM(*shape) for shape in scratch],
        compiler_params=grant(*scratch, *held),
        name="stage_two",
    )(cand, *one, median, *given)


def finish(own, moved, sums, lines, bands):
    pixels = own.shape[1]

    def kernel(own_ref, moved_ref, inner_ref, ends_ref, best_out, sinr_out, part_out):
        me, _ = places()
        level = me // lines
        inner = (level == 1) | (level == 2)
        at = jnp.where(level < 2, level, level - 2)
        here = jnp.full((1, pixels), jnp.where(inner, 1, 0), jnp.int32) != 0
        best = jnp.where(here, own_ref[0:1], moved_ref[0:1])
        other = jnp.where(here, inner_ref[pl.ds(at, 1)], ends_ref[pl.ds(at, 1)])
        total = jnp.where(here, own_ref[1:2], moved_ref[1:2]) + other
        scale = 1.0 / math.log(10.0)
        sinr = jnp.log(best / total) * scale
        best_out[...] = jnp.log(best) * scale
        sinr_out[...] = sinr
        mean = jnp.sum(sinr, axis=1, keepdims=True) / float(pixels * bands)
        part_out[...] = jnp.broadcast_to(mean, part_out.shape)

    shapes = [(1, pixels), (1, pixels), (1, 128)]
    return pl.pallas_call(
        kernel,
        in_specs=[VMEM] * 4,
        out_specs=[VMEM] * 3,
        out_shape=[jax.ShapeDtypeStruct(shape, F32) for shape in shapes],
        compiler_params=grant(*[(shape, F32) for shape in shapes]),
        name="finish",
    )(own, moved, *sums)


def plan_of(n, lead):
    half, lines = n // 2, n // 4
    row = lambda s, k: s // lines * lines + (s % lines ^ k)
    cross = lambda s, k: half - lead <= row(s, k) < half + lead
    middle = {k: [s for s in range(n) if s // lines in (1, 2) and cross(s, k)] for k in range(lines)}
    outer = {k: [s for s in range(n) if s // lines in (0, 3) and cross(s, k)] for k in range(lines)}
    return middle, outer


def shards(fields, factor, pattern, tx_power, site_position, candidates):
    _, tiles, pixels = fields.shape
    depth = factor.shape[1]
    n, bands = lax.axis_size("site"), lax.axis_size("band")
    half, lines, lead = n // 2, n // 4, depth - 1
    assert tiles == n and half >= lead
    height = tiles // 8
    middle, outer = plan_of(n, lead)
    level = lax.axis_index("site") // lines

    def swap(x, k, axis="site", sources=None):
        count = n if axis == "site" else bands
        sources = range(count) if sources is None else sources
        return lax.ppermute(x, axis, [(s, s ^ k) for s in sources])

    class0, class1, own_part = split_tiles(fields, factor, pattern, lines)

    pass_on = {0: class1[0]}
    pass_on.update({k: swap(class1[k], k) for k in range(1, lines)})
    held = {0: class0[0]}
    held.update({k: swap(class0[k], k) for k in range(1, lines)})
    far = [(3 * lines ^ k, swap(pass_on[k], 3 * lines, sources=middle[k])) for k in range(lines) if middle[k]]
    partner = [swap(pass_on[k], lines) for k in range(lines)]
    far += [(2 * lines ^ k, swap(held[k], 2 * lines, sources=outer[k])) for k in range(lines) if outer[k]]

    line_part = jnp.stack([own_part] + [swap(own_part, k) for k in range(1, lines)])
    senders = [None, range(2 * lines, 3 * lines), range(3 * lines, n)]
    order = [1, 3, 2]
    level_parts = {e: swap(line_part, e * lines, sources=some) for e, some in zip(order, senders)}
    mine = jnp.stack([line_part] + [level_parts[e] for e in range(1, 4)])[None]
    pieces = [mine, swap(mine, 1, axis="band")]

    near_cand = swap(candidates, lines)
    cand = jnp.where(level % 2 == 1, jnp.concatenate([near_cand, candidates]), jnp.concatenate([candidates, near_cand]))
    table, median, here = reach_tables(tx_power.reshape(1, -1), site_position, held[0], half, depth, pixels, height)
    one = stage_one(cand, table, pieces, [here] + [held[k] for k in range(1, lines)], partner, half, depth)
    ends = [s for s in range(n) if s // lines in (0, 3)]
    inner = [s for s in range(n) if s // lines in (1, 2)]
    sums = [swap(one[0], 2 * lines, sources=ends), swap(one[0], 3 * lines, sources=ends)]
    own, hop = stage_two(cand, one, median, far, half, depth)
    moved = swap(hop, lines, sources=inner)
    best_level, sinr_level, share = finish(own, moved, sums, lines, bands)
    bit = 1
    while bit < bands:
        share = share + swap(share, bit, axis="band")
        bit *= 2
    return best_level, sinr_level, share[0, :1]


def solution(mesh):
    placed = (
        P("site", None, "band"),
        P("site", None, None),
        P("site", None),
        P(),
        P(),
        P("site", None),
    )

    return jax.shard_map(
        shards,
        mesh=mesh,
        in_specs=placed,
        out_specs=(P("site", "band"), P("site", "band"), P("site")),
        check_vma=False,
    )
```

profile of v0, /device:TPU:0, one launch (start us, length us, event | category | flops | bytes accessed | tf_op | source)
XLA Modules:
  0.0 99.5 jit_solution(9082758562257895703)
XLA Ops:
  0.6 0.0 copy-start.7
  0.6 0.0 copy-start.6
  0.7 0.0 copy-start.5
  0.7 4.5 %split_tiles.1 = (bf16[2,128,1024]{2,1,0:T(8,128)(2,1)}, bf16[2,128,1024]{2,1,0:T(8,128)(2,1)}, bf16[2,128,1024]{2,1,0:T(8,128)(2,1)}, bf16[2,128,1024]{2,1,0:T(8,128)(2,1)}, bf16[64,512]{1,0:T(8,128)(2,1)}) custom-call(s32[1,3]{1,0:T(1,128)} %pattern_ref.1, bf16[128,8,1024]{2,1,0:T(8,128)(2,1)} %x_ref.1, bf16[128,4,128]{2,1,0:T(4,128)(2,1)} %factor_ref.1), custom_call_target="tpu_custom_call" | custom-call | tf_op jit(solution)/shard_map/split_tiles/pallas_call | solution.py:86
  5.2 3.0 %collective-permute-start.1 = (bf16[64,512]{1,0:T(8,128)(2,1)}, bf16[64,512]{1,0:T(8,128)(2,1)S(1)}, u32[]{:S(2)}, u32[]{:S(2)}) collective-permute-start(bf16[64,512]{1,0:T(8,128)(2,1)} %get-tuple-element.22), channel_id=1, source_target_pairs={{0,4},{4,0},{8,12},{12,8},{16,20},{20,16},{24,28},{28,24},{1,5},{5... | collective-permute-start | bytes 196616 | tf_op jit(solution)/shard_map/ppermute | solution.py:461
  8.2 2.5 %collective-permute-done.1 = bf16[64,512]{1,0:T(8,128)(2,1)S(1)} collective-permute-done((bf16[64,512]{1,0:T(8,128)(2,1)}, bf16[64,512]{1,0:T(8,128)(2,1)S(1)}, u32[]{:S(2)}, u32[]{:S(2)}) %collective-permute-start.1) | collective-permute-done | bytes 65568 | tf_op jit(solution)/shard_map/ppermute | solution.py:461
  10.7 0.9 fusion
  11.5 2.2 %collective-permute-start.2 = (bf16[2,64,512]{2,1,0:T(8,128)(2,1)S(1)}, bf16[2,64,512]{2,1,0:T(8,128)(2,1)S(1)}, u32[]{:S(2)}, u32[]{:S(2)}) collective-permute-start(bf16[2,64,512]{2,1,0:T(8,128)(2,1)S(1)} %get-tuple-element.38), channel_id=1, source_target_pairs={{0,8},{4,12},{8,0},{12,4},{16,24},{20,28},{24,16},{28,20},{1,9},{5... | collective-permute-start | bytes 393224 | tf_op jit(solution)/shard_map/ppermute | solution.py:461
  13.7 0.7 collective-permute-start.3
  14.4 0.7 collective-permute-start.4
  15.0 1.6 %collective-permute-start.8 = (bf16[2,128,1024]{2,1,0:T(8,128)(2,1)}, bf16[2,128,1024]{2,1,0:T(8,128)(2,1)}, u32[]{:S(2)}, u32[]{:S(2)}) collective-permute-start(bf16[2,128,1024]{2,1,0:T(8,128)(2,1)} %get-tuple-element.26), channel_id=1, source_target_pairs={{0,4},{4,0},{8,12},{12,8},{16,20},{20,16},{24,28},{28,24},{1,5},{5... | collective-permute-start | bytes 1572872 | tf_op jit(solution)/shard_map/ppermute | solution.py:461
  16.6 0.5 collective-permute-start.6
  17.1 0.0 collective-permute-done.2
  17.1 1.5 %collective-permute-start.7 = (bf16[2,128,1024]{2,1,0:T(8,128)(2,1)}, bf16[2,128,1024]{2,1,0:T(8,128)(2,1)S(1)}, u32[]{:S(2)}, u32[]{:S(2)}) collective-permute-start(bf16[2,128,1024]{2,1,0:T(8,128)(2,1)} %get-tuple-element.25), channel_id=1, source_target_pairs={{0,8},{4,12},{8,0},{12,4},{16,24},{20,28},{24,16},{28,20},{1,9},{5... | collective-permute-start | bytes 1572872 | tf_op jit(solution)/shard_map/ppermute | solution.py:461
  18.7 0.0 collective-permute-done.3
  18.7 0.0 collective-permute-done.4
  18.7 0.1 maximum_bitcast_fusion.refs_0_
  18.8 0.1 collective-permute-start.5
  18.8 11.4 %collective-permute-done.8 = bf16[2,128,1024]{2,1,0:T(8,128)(2,1)} collective-permute-done((bf16[2,128,1024]{2,1,0:T(8,128)(2,1)}, bf16[2,128,1024]{2,1,0:T(8,128)(2,1)}, u32[]{:S(2)}, u32[]{:S(2)}) %collective-permute-start.8) | collective-permute-done | bytes 524320 | tf_op jit(solution)/shard_map/ppermute | solution.py:461
  30.2 1.3 %collective-permute-start.9 = (bf16[2,128,1024]{2,1,0:T(8,128)(2,1)}, bf16[2,128,1024]{2,1,0:T(8,128)(2,1)}, u32[]{:S(2)}, u32[]{:S(2)}) collective-permute-start(bf16[2,128,1024]{2,1,0:T(8,128)(2,1)} %collective-permute-done.8), channel_id=1, source_target_pairs={{0,8},{4,12},{8,0},{12,4},{16,24},{20,28},{24,16},{28,20},{1,9},{5... | collective-permute-start | bytes 1572872 | tf_op jit(solution)/shard_map/ppermute | solution.py:461
  31.5 0.0 copy-done.7
  31.5 0.8 collective-permute-start
  32.3 8.1 %collective-permute-done = s32[1,16]{1,0:T(1,128)S(1)} collective-permute-done((s32[1,16]{1,0:T(1,128)S(1)}, s32[1,16]{1,0:T(1,128)S(1)}, u32[]{:S(2)}, u32[]{:S(2)}) %collective-permute-start) | collective-permute-done | bytes 96 | tf_op jit(solution)/shard_map/ppermute | solution.py:461
  40.4 0.7 collective-permute-start.10
  41.1 0.0 collective-permute-done.6.refs_3_
  41.1 0.7 collective-permute-start.12
  41.8 0.0 collective-permute-done.7.refs_4_
  41.8 0.0 copy-start.1
  41.8 0.8 copy-done.1
  42.6 0.7 collective-permute-start.11
  43.3 0.0 collective-permute-done.5.refs_1_
  43.3 0.0 copy-start.3
  43.3 0.8 copy-done.3
  44.1 11.2 %collective-permute-start.13 = (bf16[2,128,1024]{2,1,0:T(8,128)(2,1)S(1)}, bf16[2,128,1024]{2,1,0:T(8,128)(2,1)S(1)}, u32[]{:S(2)}, u32[]{:S(2)}) collective-permute-start(bf16[2,128,1024]{2,1,0:T(8,128)(2,1)S(1)} %collective-permute-done.6.refs_3_), channel_id=1, source_target_pairs={{0,16},{28,12},{1,17},{29,13},{2,18},{30,14},{3,19},{31,15}} | collective-permute-start | bytes 1572872 | tf_op jit(solution)/shard_map/ppermute | solution.py:461
  55.3 0.0 copy-done.6
  55.3 0.0 copy-done.5
  55.3 0.0 copy-start
  55.3 1.0 %copy-done = bf16[2,128,1024]{2,1,0:T(8,128)(2,1)S(1)} copy-done((bf16[2,128,1024]{2,1,0:T(8,128)(2,1)S(1)}, bf16[2,128,1024]{2,1,0:T(8,128)(2,1)}, u32[]{:S(2)}) %copy-start) | copy-done | bytes 524312
  56.4 1.4 %reach_tables.1 = (f32[2,512,1024]{2,1,0:T(8,128)S(1)}, f32[2,384,1024]{2,1,0:T(8,128)S(1)}, bf16[2,128,1024]{2,1,0:T(8,128)(2,1)S(1)}) custom-call(f32[1,1024]{1,0:T(1,128)S(1)} %bitcast.12, f32[2,1024]{1,0:T(2,128)S(1)} %copy-done.5, bf16[2,128,1024]{2,1,0:T(8,128)(2,1)S(1)} %copy-done), custom_call_target="tpu_custom_call" | custom-call | flops 36700160 | bytes 8388608 | tf_op jit(solution)/shard_map/reach_tables/pallas_call | solution.py:193
  57.8 0.0 collective-permute-done.9.refs_5_
  57.8 0.0 copy-start.2
  57.8 1.0 %copy-done.2 = bf16[2,128,1024]{2,1,0:T(8,128)(2,1)S(1)} copy-done((bf16[2,128,1024]{2,1,0:T(8,128)(2,1)S(1)}, bf16[2,128,1024]{2,1,0:T(8,128)(2,1)}, u32[]{:S(2)}) %copy-start.2) | copy-done | bytes 524312
  58.8 0.0 copy-start.4
  58.8 1.0 %copy-done.4 = bf16[1,4,2,64,512]{4,3,2,1,0:T(8,128)(2,1)S(1)} copy-done((bf16[1,4,2,64,512]{4,3,2,1,0:T(8,128)(2,1)S(1)}, bf16[1,4,2,64,512]{4,3,2,1,0:T(8,128)(2,1)}, u32[]{:S(2)}) %copy-start.4) | copy-done | bytes 524312
  59.9 5.4 %stage_one.1 = (f32[2,1024]{1,0:T(2,128)S(1)}, f32[2,1024]{1,0:T(2,128)S(1)}, f32[2,384,1024]{2,1,0:T(8,128)S(1)}, bf16[384,384]{1,0:T(8,128)(2,1)S(1)}) custom-call(s32[2,16]{1,0:T(2,128)S(1)} %add_select_fusion.cand_ref, f32[2,512,1024]{2,1,0:T(8,128)S(1)} %get-tuple-element.21.table_ref, bf16[1,4,2,64,512]{4,3,2,1,0:T(8,128)(2,1)S(1)} %maximum_bitcast_fusion.refs_0_, ...), custom_call_target="tpu_custom_call" | custom-call | flops 1476395008 | bytes 8388608 | tf_op jit(solution)/shard_map/stage_one/pallas_call | solution.py:327
  65.2 0.0 collective-permute-done.10.refs_0_
  65.2 0.0 collective-permute-done.12.refs_2_
  65.2 0.0 collective-permute-done.11.refs_1_
  65.2 0.0 collective-permute-done.13.refs_3_
  65.3 0.6 stage_two.1
  65.8 1.3 %collective-permute-start.14 = (f32[2,1024]{1,0:T(2,128)S(1)}, f32[2,1024]{1,0:T(2,128)S(1)}, u32[]{:S(2)}, u32[]{:S(2)}) collective-permute-start(f32[2,1024]{1,0:T(2,128)S(1)} %get-tuple-element.33), channel_id=1, source_target_pairs={{8,0},{12,4},{16,24},{20,28},{9,1},{13,5},{17,25},{21,29},{10,2},{... | collective-permute-start | bytes 24584 | tf_op jit(solution)/shard_map/ppermute | solution.py:461
  67.1 19.1 %collective-permute-start.15 = (f32[2,1024]{1,0:T(2,128)S(1)}, f32[2,1024]{1,0:T(2,128)S(1)}, u32[]{:S(2)}, u32[]{:S(2)}) collective-permute-start(f32[2,1024]{1,0:T(2,128)S(1)} %get-tuple-element.27.sums), channel_id=1, source_target_pairs={{0,16},{4,20},{24,8},{28,12},{1,17},{5,21},{25,9},{29,13},{2,18},{... | collective-permute-start | bytes 24584 | tf_op jit(solution)/shard_map/ppermute | solution.py:461
  86.3 2.7 %collective-permute-start.16 = (f32[2,1024]{1,0:T(2,128)S(1)}, f32[2,1024]{1,0:T(2,128)S(1)}, u32[]{:S(2)}, u32[]{:S(2)}) collective-permute-start(f32[2,1024]{1,0:T(2,128)S(1)} %get-tuple-element.27.sums), channel_id=1, source_target_pairs={{0,24},{4,28},{24,0},{28,4},{1,25},{5,29},{25,1},{29,5},{2,26},{6,... | collective-permute-start | bytes 24584 | tf_op jit(solution)/shard_map/ppermute | solution.py:461
  89.0 0.0 collective-permute-done.14.moved_ref
  89.0 0.0 collective-permute-done.15.inner_ref
  89.0 4.6 %collective-permute-done.16.ends_ref = f32[2,1024]{1,0:T(2,128)S(1)} collective-permute-done((f32[2,1024]{1,0:T(2,128)S(1)}, f32[2,1024]{1,0:T(2,128)S(1)}, u32[]{:S(2)}, u32[]{:S(2)}) %collective-permute-start.16) | collective-permute-done | bytes 8224 | tf_op jit(solution)/shard_map/ppermute | solution.py:461
  93.6 0.6 finish.1
  94.2 0.0 collective-permute-start.17
  94.2 1.2 %collective-permute-done.17 = f32[1,128]{1,0:T(1,128)S(1)} collective-permute-done((f32[1,128]{1,0:T(1,128)S(1)}, f32[1,128]{1,0:T(1,128)S(1)}, u32[]{:S(2)}, u32[]{:S(2)}) %collective-permute-start.17) | collective-permute-done | bytes 544 | tf_op jit(solution)/shard_map/ppermute | solution.py:461
  95.4 1.4 %collective-permute-start.18 = (f32[1,128]{1,0:T(1,128)S(1)}, f32[1,128]{1,0:T(1,128)S(1)}, u32[]{:S(2)}, u32[]{:S(2)}) collective-permute-start(f32[1,128]{1,0:T(1,128)S(1)} %add.12), channel_id=1, source_target_pairs={{0,2},{1,3},{2,0},{3,1},{4,6},{5,7},{6,4},{7,5},{8,10},{9,11},{10,... | collective-permute-start | bytes 1544 | tf_op jit(solution)/shard_map/ppermute | solution.py:461
  96.8 2.2 %collective-permute-done.18 = f32[1,128]{1,0:T(1,128)S(1)} collective-permute-done((f32[1,128]{1,0:T(1,128)S(1)}, f32[1,128]{1,0:T(1,128)S(1)}, u32[]{:S(2)}, u32[]{:S(2)}) %collective-permute-start.18) | collective-permute-done | bytes 544 | tf_op jit(solution)/shard_map/ppermute | solution.py:461
  99.0 0.5 add.13
  (2 shorter events, 0.0 us)
Async XLA Ops:
  0.6 30.9 %copy-start.7 = (s32[1,16]{1,0:T(1,128)S(1)}, s32[1,16]{1,0:T(1,128)}, u32[]{:S(2)}) copy-start(s32[1,16]{1,0:T(1,128)} %param.11) | copy-start | bytes 196
  0.6 54.7 %copy-start.6 = (f32[1024]{0:T(1024)S(1)}, f32[1024]{0:T(1024)}, u32[]{:S(2)}) copy-start(f32[1024]{0:T(1024)} %param.9) | copy-start | bytes 12292
  0.7 54.7 %copy-start.5 = (f32[2,1024]{1,0:T(2,128)S(1)}, f32[2,1024]{1,0:T(2,128)}, u32[]{:S(2)}) copy-start(f32[2,1024]{1,0:T(2,128)} %pos_ref.1) | copy-start | bytes 24580
  5.2 5.5 %collective-permute-start.1 = (bf16[64,512]{1,0:T(8,128)(2,1)}, bf16[64,512]{1,0:T(8,128)(2,1)S(1)}, u32[]{:S(2)}, u32[]{:S(2)}) collective-permute-start(bf16[64,512]{1,0:T(8,128)(2,1)} %get-tuple-element.22), channel_id=1, source_target_pairs={{0,4},{4,0},{8,12},{12,8},{16,20},{20,16},{24,28},{28,24},{1,5},{5... | collective-permute-start | bytes 196616 | tf_op jit(solution)/shard_map/ppermute | solution.py:461
  11.5 5.6 %collective-permute-start.2 = (bf16[2,64,512]{2,1,0:T(8,128)(2,1)S(1)}, bf16[2,64,512]{2,1,0:T(8,128)(2,1)S(1)}, u32[]{:S(2)}, u32[]{:S(2)}) collective-permute-start(bf16[2,64,512]{2,1,0:T(8,128)(2,1)S(1)} %get-tuple-element.38), channel_id=1, source_target_pairs={{0,8},{4,12},{8,0},{12,4},{16,24},{20,28},{24,16},{28,20},{1,9},{5... | collective-permute-start | bytes 393224 | tf_op jit(solution)/shard_map/ppermute | solution.py:461
  13.7 5.0 %collective-permute-start.3 = (bf16[2,64,512]{2,1,0:T(8,128)(2,1)S(1)}, bf16[2,64,512]{2,1,0:T(8,128)(2,1)S(1)}, u32[]{:S(2)}, u32[]{:S(2)}) collective-permute-start(bf16[2,64,512]{2,1,0:T(8,128)(2,1)S(1)} %get-tuple-element.38), channel_id=1, source_target_pairs={{24,8},{28,12},{25,9},{29,13},{26,10},{30,14},{27,11},{31,15}} | collective-permute-start | bytes 393224 | tf_op jit(solution)/shard_map/ppermute | solution.py:461
  14.4 4.3 %collective-permute-start.4 = (bf16[2,64,512]{2,1,0:T(8,128)(2,1)S(1)}, bf16[2,64,512]{2,1,0:T(8,128)(2,1)S(1)}, u32[]{:S(2)}, u32[]{:S(2)}) collective-permute-start(bf16[2,64,512]{2,1,0:T(8,128)(2,1)S(1)} %get-tuple-element.38), channel_id=1, source_target_pairs={{16,8},{20,12},{17,9},{21,13},{18,10},{22,14},{19,11},{23,15}} | collective-permute-start | bytes 393224 | tf_op jit(solution)/shard_map/ppermute | solution.py:461
  15.0 15.2 %collective-permute-start.8 = (bf16[2,128,1024]{2,1,0:T(8,128)(2,1)}, bf16[2,128,1024]{2,1,0:T(8,128)(2,1)}, u32[]{:S(2)}, u32[]{:S(2)}) collective-permute-start(bf16[2,128,1024]{2,1,0:T(8,128)(2,1)} %get-tuple-element.26), channel_id=1, source_target_pairs={{0,4},{4,0},{8,12},{12,8},{16,20},{20,16},{24,28},{28,24},{1,5},{5... | collective-permute-start | bytes 1572872 | tf_op jit(solution)/shard_map/ppermute | solution.py:461
  16.6 24.5 %collective-permute-start.6 = (bf16[2,128,1024]{2,1,0:T(8,128)(2,1)}, bf16[2,128,1024]{2,1,0:T(8,128)(2,1)S(1)}, u32[]{:S(2)}, u32[]{:S(2)}) collective-permute-start(bf16[2,128,1024]{2,1,0:T(8,128)(2,1)} %get-tuple-element.24), channel_id=1, source_target_pairs={{0,4},{4,0},{8,12},{12,8},{16,20},{20,16},{24,28},{28,24},{1,5},{5... | collective-permute-start | bytes 1572872 | tf_op jit(solution)/shard_map/ppermute | solution.py:461
  17.1 24.6 %collective-permute-start.7 = (bf16[2,128,1024]{2,1,0:T(8,128)(2,1)}, bf16[2,128,1024]{2,1,0:T(8,128)(2,1)S(1)}, u32[]{:S(2)}, u32[]{:S(2)}) collective-permute-start(bf16[2,128,1024]{2,1,0:T(8,128)(2,1)} %get-tuple-element.25), channel_id=1, source_target_pairs={{0,8},{4,12},{8,0},{12,4},{16,24},{20,28},{24,16},{28,20},{1,9},{5... | collective-permute-start | bytes 1572872 | tf_op jit(solution)/shard_map/ppermute | solution.py:461
  18.8 24.5 %collective-permute-start.5 = (bf16[1,4,2,64,512]{4,3,2,1,0:T(8,128)(2,1)S(1)}, bf16[1,4,2,64,512]{4,3,2,1,0:T(8,128)(2,1)S(1)}, u32[]{:S(2)}, u32[]{:S(2)}) collective-permute-start(bf16[1,4,2,64,512]{4,3,2,1,0:T(8,128)(2,1)S(1)} %maximum_bitcast_fusion.refs_0_), channel_id=1, source_target_pairs={{0,1},{1,0},{2,3},{3,2},{4,5},{5,4},{6,7},{7,6},{8,9},{9,8},{10,11... | collective-permute-start | bytes 1572872 | tf_op jit(solution)/shard_map/ppermute | solution.py:461
  30.2 27.5 %collective-permute-start.9 = (bf16[2,128,1024]{2,1,0:T(8,128)(2,1)}, bf16[2,128,1024]{2,1,0:T(8,128)(2,1)}, u32[]{:S(2)}, u32[]{:S(2)}) collective-permute-start(bf16[2,128,1024]{2,1,0:T(8,128)(2,1)} %collective-permute-done.8), channel_id=1, source_target_pairs={{0,8},{4,12},{8,0},{12,4},{16,24},{20,28},{24,16},{28,20},{1,9},{5... | collective-permute-start | bytes 1572872 | tf_op jit(solution)/shard_map/ppermute | solution.py:461
  31.5 8.9 %collective-permute-start = (s32[1,16]{1,0:T(1,128)S(1)}, s32[1,16]{1,0:T(1,128)S(1)}, u32[]{:S(2)}, u32[]{:S(2)}) collective-permute-start(s32[1,16]{1,0:T(1,128)S(1)} %copy-done.7), channel_id=1, source_target_pairs={{0,8},{4,12},{8,0},{12,4},{16,24},{20,28},{24,16},{28,20},{1,9},{5... | collective-permute-start | bytes 200 | tf_op jit(solution)/shard_map/ppermute | solution.py:461
  40.4 24.8 %collective-permute-start.10 = (bf16[2,128,1024]{2,1,0:T(8,128)(2,1)}, bf16[2,128,1024]{2,1,0:T(8,128)(2,1)S(1)}, u32[]{:S(2)}, u32[]{:S(2)}) collective-permute-start(bf16[2,128,1024]{2,1,0:T(8,128)(2,1)} %get-tuple-element.25), channel_id=1, source_target_pairs={{8,16},{12,20},{16,8},{20,12},{9,17},{13,21},{17,9},{21,13},{10,18... | collective-permute-start | bytes 1572872 | tf_op jit(solution)/shard_map/ppermute | solution.py:461
  41.1 24.2 %collective-permute-start.12 = (bf16[2,128,1024]{2,1,0:T(8,128)(2,1)}, bf16[2,128,1024]{2,1,0:T(8,128)(2,1)S(1)}, u32[]{:S(2)}, u32[]{:S(2)}) collective-permute-start(bf16[2,128,1024]{2,1,0:T(8,128)(2,1)} %get-tuple-element.20.unit_ref), channel_id=1, source_target_pairs={{4,20},{24,8},{5,21},{25,9},{6,22},{26,10},{7,23},{27,11}} | collective-permute-start | bytes 1572872 | tf_op jit(solution)/shard_map/ppermute | solution.py:461
  41.8 0.8 copy-start.1
  42.6 22.7 %collective-permute-start.11 = (bf16[2,128,1024]{2,1,0:T(8,128)(2,1)}, bf16[2,128,1024]{2,1,0:T(8,128)(2,1)S(1)}, u32[]{:S(2)}, u32[]{:S(2)}) collective-permute-start(bf16[2,128,1024]{2,1,0:T(8,128)(2,1)} %collective-permute-done.8), channel_id=1, source_target_pairs={{8,16},{12,20},{16,8},{20,12},{9,17},{13,21},{17,9},{21,13},{10,18... | collective-permute-start | bytes 1572872 | tf_op jit(solution)/shard_map/ppermute | solution.py:461
  43.3 0.8 copy-start.3
  44.1 21.2 %collective-permute-start.13 = (bf16[2,128,1024]{2,1,0:T(8,128)(2,1)S(1)}, bf16[2,128,1024]{2,1,0:T(8,128)(2,1)S(1)}, u32[]{:S(2)}, u32[]{:S(2)}) collective-permute-start(bf16[2,128,1024]{2,1,0:T(8,128)(2,1)S(1)} %collective-permute-done.6.refs_3_), channel_id=1, source_target_pairs={{0,16},{28,12},{1,17},{29,13},{2,18},{30,14},{3,19},{31,15}} | collective-permute-start | bytes 1572872 | tf_op jit(solution)/shard_map/ppermute | solution.py:461
  55.3 1.0 %copy-start = (bf16[2,128,1024]{2,1,0:T(8,128)(2,1)S(1)}, bf16[2,128,1024]{2,1,0:T(8,128)(2,1)}, u32[]{:S(2)}) copy-start(bf16[2,128,1024]{2,1,0:T(8,128)(2,1)} %get-tuple-element.20.unit_ref) | copy-start | bytes 1572868
  57.8 1.0 %copy-start.2 = (bf16[2,128,1024]{2,1,0:T(8,128)(2,1)S(1)}, bf16[2,128,1024]{2,1,0:T(8,128)(2,1)}, u32[]{:S(2)}) copy-start(bf16[2,128,1024]{2,1,0:T(8,128)(2,1)} %copy-done.1) | copy-start | bytes 1572868
  58.8 1.0 %copy-start.4 = (bf16[1,4,2,64,512]{4,3,2,1,0:T(8,128)(2,1)S(1)}, bf16[1,4,2,64,512]{4,3,2,1,0:T(8,128)(2,1)}, u32[]{:S(2)}) copy-start(bf16[1,4,2,64,512]{4,3,2,1,0:T(8,128)(2,1)} %copy-done.3) | copy-start | bytes 1572868
  65.8 23.2 %collective-permute-start.14 = (f32[2,1024]{1,0:T(2,128)S(1)}, f32[2,1024]{1,0:T(2,128)S(1)}, u32[]{:S(2)}, u32[]{:S(2)}) collective-permute-start(f32[2,1024]{1,0:T(2,128)S(1)} %get-tuple-element.33), channel_id=1, source_target_pairs={{8,0},{12,4},{16,24},{20,28},{9,1},{13,5},{17,25},{21,29},{10,2},{... | collective-permute-start | bytes 24584 | tf_op jit(solution)/shard_map/ppermute | solution.py:461
  67.1 21.9 %collective-permute-start.15 = (f32[2,1024]{1,0:T(2,128)S(1)}, f32[2,1024]{1,0:T(2,128)S(1)}, u32[]{:S(2)}, u32[]{:S(2)}) collective-permute-start(f32[2,1024]{1,0:T(2,128)S(1)} %get-tuple-element.27.sums), channel_id=1, source_target_pairs={{0,16},{4,20},{24,8},{28,12},{1,17},{5,21},{25,9},{29,13},{2,18},{... | collective-permute-start | bytes 24584 | tf_op jit(solution)/shard_map/ppermute | solution.py:461
  86.3 7.3 %collective-permute-start.16 = (f32[2,1024]{1,0:T(2,128)S(1)}, f32[2,1024]{1,0:T(2,128)S(1)}, u32[]{:S(2)}, u32[]{:S(2)}) collective-permute-start(f32[2,1024]{1,0:T(2,128)S(1)} %get-tuple-element.27.sums), channel_id=1, source_target_pairs={{0,24},{4,28},{24,0},{28,4},{1,25},{5,29},{25,1},{29,5},{2,26},{6,... | collective-permute-start | bytes 24584 | tf_op jit(solution)/shard_map/ppermute | solution.py:461
  94.2 1.2 %collective-permute-start.17 = (f32[1,128]{1,0:T(1,128)S(1)}, f32[1,128]{1,0:T(1,128)S(1)}, u32[]{:S(2)}, u32[]{:S(2)}) collective-permute-start(f32[1,128]{1,0:T(1,128)S(1)} %get-tuple-element.36), channel_id=1, source_target_pairs={{0,1},{1,0},{2,3},{3,2},{4,5},{5,4},{6,7},{7,6},{8,9},{9,8},{10,11... | collective-permute-start | bytes 1544 | tf_op jit(solution)/shard_map/ppermute | solution.py:461
  95.4 3.6 %collective-permute-start.18 = (f32[1,128]{1,0:T(1,128)S(1)}, f32[1,128]{1,0:T(1,128)S(1)}, u32[]{:S(2)}, u32[]{:S(2)}) collective-permute-start(f32[1,128]{1,0:T(1,128)S(1)} %add.12), channel_id=1, source_target_pairs={{0,2},{1,3},{2,0},{3,1},{4,6},{5,7},{6,4},{7,5},{8,10},{9,11},{10,... | collective-permute-start | bytes 1544 | tf_op jit(solution)/shard_map/ppermute | solution.py:461
where the time goes:
time: 100 us; the launch traced here: 99.5 us
  starting transfers between devices  50 us (50%)
  waiting for transfers between devices  29.9 us (30%)
  Pallas kernels  12.4 us (12%)
  local copies, waits for them, and re-layouts  4.69 us (5%)
  other arithmetic  1.45 us (1%)
    ppermute x19, starting transfers between devices, swap(): return lax.ppermute(x, axis, [(s, s ^ k) for s in sources])  50 us
    ppermute x19, waiting for transfers between devices, swap(): return lax.ppermute(x, axis, [(s, s ^ k) for s in sources])  29.9 us
    pallas_call x1, Pallas kernels, stage_one(): pl.pallas_call(kernel, in_specs=[SMEM] + [VMEM] * len(given), out_specs=[...  5.36 us
    unnamed x16, local copies, waits for them, and re-layouts  4.69 us
    pallas_call x1, Pallas kernels, split_tiles(): pl.pallas_call(kernel, in_specs=[SMEM, HBM, HBM], out_specs=[VMEM] * (np_...  4.52 us
  transfers between devices with their start and end apart: 19, of which 6 were waited for; matrix products, arithmetic and copies ran while one was open for 0% of the time, Pallas kernels for 7%

commit v1 on v0

v1 whole, which is shorter than its diff:
```python
import functools
import math

import jax
import jax.numpy as jnp
from jax import lax
from jax.experimental import pallas as pl
from jax.experimental.pallas import tpu as pltpu
from jax.sharding import PartitionSpec as P


COLS = 256
spacing = 0.03
ln_tenth = 0.2302585093
to_exp2 = ln_tenth * math.log2(math.e)
dist_gain = to_exp2 * 11.0 * math.log10(2.0)
mixed_gain = to_exp2 * 8.0
F32 = jnp.float32
BF16 = jnp.bfloat16
SHARES = 2
HBM = pl.BlockSpec(memory_space=pltpu.HBM)
SMEM = pl.BlockSpec(memory_space=pltpu.SMEM)
VMEM = pl.BlockSpec(memory_space=pltpu.VMEM)


def places():
    return lax.axis_index("site"), lax.axis_index("band")


def grant(*parts):
    size = sum(math.prod(shape) * jnp.dtype(kind).itemsize for shape, kind in parts)
    return pltpu.CompilerParams(vmem_limit_bytes=min(size + (8 << 20), 60 << 20))


def split_tiles(fields, factor, pattern, lines):
    block, tiles, pixels = fields.shape
    depth = factor.shape[1]
    chunk = min(block, max(1, 256 // tiles))
    part = block // SHARES
    wide = depth * block

    steps = block // chunk

    def kernel(pattern_ref, x_ref, factor_ref, *refs):
        outs, (coef_out, x_in, factor_in, pattern_in, sems) = refs[: 3 * lines], refs[3 * lines :]
        me, band = places()
        copies = [pltpu.make_async_copy(factor_ref.at[pl.ds(band % SHARES * part, part)], factor_in, sems.at[steps])]
        for i in range(steps):
            span = slice(i * chunk, (i + 1) * chunk)
            copies.append(pltpu.make_async_copy(x_ref.at[span], x_in.at[span], sems.at[i]))
        copies.append(pltpu.make_async_copy(pattern_ref, pattern_in, sems.at[steps + 1]))
        for copy in copies:
            copy.start()
        size = chunk * tiles
        row = lax.broadcasted_iota(jnp.int32, (size, size), 0)
        col = lax.broadcasted_iota(jnp.int32, (size, size), 1)
        slot = row // chunk
        kind, k, j = slot // (2 * lines), slot // 2 % lines, slot % 2
        second = ((me // lines) & 1) ^ 1 ^ kind
        tile = jnp.where(second == 1, 3 - j, j) * lines + ((me % lines) ^ k)
        move = jnp.where(col == row % chunk * tiles + tile, 1.0, 0.0)
        copies[0].wait()
        copies[-1].wait()
        row = lax.broadcasted_iota(jnp.int32, (part, block), 0) + band % SHARES * part
        col = lax.broadcasted_iota(jnp.int32, (part, block), 1)
        rows = factor_in[...].astype(F32)
        for d in range(depth):
            keep = col <= row if d == 0 else jnp.full((part, block), pattern_in[0, d - 1], jnp.int32) != 0
            lane = (depth - 1 - d) * block
            coef_out[:, lane : lane + block] = jnp.where(keep, rows[:, d, :], 0.0).astype(BF16)
        for i in range(steps):
            copies[i + 1].wait()
            rows = slice(i * chunk, (i + 1) * chunk)
            for c in range(0, pixels, 256):
                span = slice(c, c + 256)
                x = x_in[rows, :, span].astype(F32).reshape(size, 256)
                moved = jnp.dot(move, x, preferred_element_type=F32).astype(BF16)
                for p in range(tiles):
                    unit = moved[p * chunk : (p + 1) * chunk]
                    if p < 2 * lines:
                        outs[p][rows, span] = unit
                    else:
                        outs[lines + p // 2][p % 2, rows, span] = unit

    shapes = [((block, pixels), BF16)] * (2 * lines) + [((2, block, pixels), BF16)] * lines + [((part, wide), BF16)]
    scratch = [((block, tiles, pixels), BF16), ((part, depth, block), BF16)]
    out = pl.pallas_call(
        kernel,
        in_specs=[HBM] * 3,
        out_specs=[VMEM] * (3 * lines + 1),
        out_shape=[jax.ShapeDtypeStruct(*shape) for shape in shapes],
        scratch_shapes=[pltpu.VMEM(*one) for one in scratch]
        + [pltpu.SMEM(pattern.shape, jnp.int32), pltpu.SemaphoreType.DMA((steps + 2,))],
        compiler_params=grant(*shapes, *scratch),
        name="split_tiles",
    )(*[pltpu.with_memory_space_constraint(x, pltpu.HBM) for x in (pattern, fields, factor)])
    first = [out[2 * k : 2 * k + 2] for k in range(lines)]
    return first, out[2 * lines : 3 * lines], out[-1]


def tile_of(me, lines, j):
    level = me // lines
    return jnp.where(level % 2 == 1, j, 3 - j) * lines + me % lines


def column(ref, row, i, block):
    line = ref[pl.ds(row, 1), pl.ds(pl.multiple_of(i * block, block), block)]
    return jnp.broadcast_to(line, (block, block)).T


def geometry(tx_ref, pos_ref, i, block, height):
    xs = column(pos_ref, 0, i, block) * (8.0 * COLS * spacing)
    ys = column(pos_ref, 1, i, block) * (height * COLS * spacing)
    base = to_exp2 * (column(tx_ref, 0, i, block) - 10.0)
    wide = COLS // block
    return jnp.concatenate([xs] * wide, axis=1), ys, jnp.concatenate([base] * wide, axis=1)


def across(xs, tile):
    col = lax.broadcasted_iota(jnp.int32, (1, COLS), 1)
    dx = xs - (tile % 8 * COLS + col).astype(F32) * spacing
    return dx * dx


def reach(dx2, ys, base, tile, row):
    at = jnp.full(ys.shape, tile // 8 * COLS + row, jnp.int32).astype(F32) * spacing
    dy = ys - at
    dy2 = dy * dy + spacing * spacing
    d2 = dx2 + jnp.concatenate([dy2] * (COLS // ys.shape[1]), axis=1)
    return base - dist_gain * jnp.log2(d2)


def rounded(mixed):
    return mixed_gain * mixed.astype(BF16).astype(F32)


def fold(power):
    return jnp.sum(power.reshape(power.shape[0] // 8, 8, power.shape[1]), axis=0)


def pick(cand_ref, j, first_site, pw, top, block):
    pixels = pw.shape[1]
    best = jnp.full((1, pixels), -1.0, F32)
    serving = jnp.zeros((1, pixels), jnp.int32)
    for c in range(cand_ref.shape[1]):
        local = jnp.clip(cand_ref[j, c] - first_site, 0, block - 1)
        power = pw[pl.ds(top + local, 1), :]
        more = power > best
        best = jnp.where(more, power, best)
        serving = jnp.where(more, local, serving)
    rest = []
    for c in range(0, pixels, COLS):
        ids = lax.broadcasted_iota(jnp.int32, (block, COLS), 0)
        mine = pw[pl.ds(top, block), c : c + COLS]
        rest.append(fold(jnp.where(ids == serving[:, c : c + COLS], 0.0, mine)))
    return best, jnp.concatenate(rest, axis=1)


def fill_table(out, tx_ref, pos_ref, place, i, half, height):
    me, band = places()
    block = tx_ref.shape[1] // (2 * half)
    pixels = out.shape[2]
    rows = pixels // COLS
    xs, ys, base = geometry(tx_ref, pos_ref, i, block, height)
    for j in range(2):
        tile = tile_of(me, half // 2, j)
        dx2 = across(xs, tile)
        for r in range(rows):
            span = slice(r * COLS, (r + 1) * COLS)
            out[j, pl.ds(place, block), span] = reach(dx2, ys, base, tile, band * rows + r)


def reach_tables(tx, pos, units, half, depth, pixels, height):
    block = tx.shape[1] // (2 * half)
    lead = depth - 1

    def kernel(tx_ref, pos_ref, unit0, unit1, table, out0, out1):
        out0[...] = unit0[...]
        out1[...] = unit1[...]
        me, _ = places()
        upper = me // half

        def body(l, carry):
            fill_table(table, tx_ref, pos_ref, pl.multiple_of(l * block, block), upper * half + l, half, height)
            return carry

        lax.fori_loop(upper * lead, half, body, 0)

    outs = [((2, half * block, pixels), F32)] + [(unit.shape, BF16) for unit in units]
    flops = 20 * 2 * half * block * pixels
    return pl.pallas_call(
        kernel,
        in_specs=[VMEM] * 4,
        out_specs=[VMEM] * 3,
        out_shape=[jax.ShapeDtypeStruct(*out) for out in outs],
        compiler_params=grant(*outs, *outs[1:]),
        cost_estimate=pl.CostEstimate(flops=flops, bytes_accessed=8 << 20, transcendentals=0),
        name="reach_tables",
    )(tx, pos, *units)


def middle_tables(tx, pos, half, depth, pixels, height):
    block = tx.shape[1] // (2 * half)
    lead, lines = depth - 1, half // 2

    def kernel(tx_ref, pos_ref, median):
        me, _ = places()
        level = me // lines

        @pl.when((level == 1) | (level == 2))
        def _():
            def body(l, carry):
                fill_table(median, tx_ref, pos_ref, pl.multiple_of(l * block, block), half + l, half, height)
                return carry

            lax.fori_loop(0, lead, body, 0)

    out = ((2, lead * block, pixels), F32)
    flops = 20 * 2 * lead * block * pixels
    return pl.pallas_call(
        kernel,
        in_specs=[VMEM] * 2,
        out_specs=VMEM,
        out_shape=jax.ShapeDtypeStruct(*out),
        compiler_params=grant(out),
        cost_estimate=pl.CostEstimate(flops=flops, bytes_accessed=4 << 20, transcendentals=0),
        name="middle_tables",
    )(tx, pos)


def stage_one(at_ends, cand, table, pieces, ends_rows, held, partner, half, depth):
    block, pixels = held[0].shape
    lead, lines = depth - 1, half // 2
    rows = pixels // COLS
    n, part, wide = 2 * half, pieces[0].shape[2], depth * block
    np_, nh = len(pieces), len(partner)
    tall = lead * block

    def kernel(cand_ref, table_ref, *refs):
        piece_refs, refs = refs[:np_], refs[np_:]
        held_refs, refs = refs[: 2 * nh], refs[2 * nh :]
        partner_refs, refs = refs[:nh], refs[nh:]
        if at_ends:
            sums, near, coef, coef_own, group, pw, acc = refs
        else:
            sums, best_out, partial, coef_cross, near, coef, coef_own, group, pw, acc = refs
        me, band = places()
        upper = me // half
        low = upper * half
        level = me // lines
        inner = (level == 1) | (level == 2)
        active = jnp.logical_not(inner) if at_ends else inner

        @pl.when(active)
        def _():
            for m, piece in enumerate(piece_refs):
                there = pl.ds(pl.multiple_of((band % SHARES ^ m) * part, part), part)
                for i, high in enumerate(ends_rows):
                    coef[3 * lines + high, there, :] = piece[3 + i, 0]
                for k in range(lines):
                    coef[me ^ 3 * lines ^ k, there, :] = piece[2, k]
                for k in range(lines):
                    coef[me ^ lines ^ k, there, :] = piece[1, k]
                    coef[me ^ k, there, :] = piece[0, k]
            near[:, :lead] = jnp.zeros((2, lead, block, pixels), BF16)
            for k in range(lines):
                for j in range(2):
                    near[j, lead + (me ^ k) - low] = held_refs[2 * k + j][...]
                    near[j, lead + (me ^ k ^ lines) - low] = partner_refs[k][j]
            acc[...] = jnp.zeros_like(acc)
            if not at_ends:
                best_out[...] = jnp.zeros_like(best_out)
                up = jnp.full((block, block), upper, jnp.int32) != 0
                for l in range(lead):
                    for c in range(lead):
                        zero = jnp.zeros((block, block), BF16)
                        early = coef[half + l, :, (c - l) * block : (c - l + 1) * block] if c >= l else zero
                        at = lead - l + c
                        late = coef[half + l, :, at * block : (at + 1) * block] if c <= l else zero
                        there = (slice(l * block, (l + 1) * block), slice(c * block, (c + 1) * block))
                        early, late = early.astype(F32), late.astype(F32)
                        coef_own[there] = jnp.where(up, late, early).astype(BF16)
                        coef_cross[there] = jnp.where(up, early, late).astype(BF16)
                top = jnp.where(upper == 0, half, lead)
                for j in range(2):
                    for r in range(rows):
                        span = slice(r * COLS, (r + 1) * COLS)
                        some = near[j, pl.ds(top, lead), :, span].reshape(tall, COLS)
                        partial[j, :, span] = jnp.dot(coef_own[...], some, preferred_element_type=F32)

            first = upper * lead

            def add(j, i, span, power):
                if at_ends:
                    acc[j, :, span] += fold(power)
                    return
                own = i == tile_of(me, lines, j)

                @pl.when(own)
                def _():
                    pw[j, :, span] = power

                acc[j, :, span] += jnp.where(own, 0.0, fold(power))

            @pl.when(upper == 0)
            def _():
                for g in range(0, half, depth):
                    count = min(depth, half - g)
                    start = max(0, g - lead)
                    deep = g + count - start
                    for a in range(count):
                        for b in range(deep):
                            d = g + a - start - b
                            there = (slice(a * block, (a + 1) * block), slice(b * block, (b + 1) * block))
                            if 0 <= d < depth:
                                group[there] = coef[g + a, :, (lead - d) * block : (depth - d) * block]
                            else:
                                group[there] = jnp.zeros((block, block), BF16)
                    for j in range(2):
                        for r in range(rows):
                            span = slice(r * COLS, (r + 1) * COLS)
                            some = near[j, lead + start : lead + start + deep, :, span].reshape(deep * block, COLS)
                            here = slice(g * block, (g + count) * block)
                            mixed = jnp.dot(group[: count * block, : deep * block], some, preferred_element_type=F32)
                            power = jnp.exp2(table_ref[j, here, span] + rounded(mixed))
                            for a in range(count):
                                add(j, g + a, span, power[a * block : (a + 1) * block])

            @pl.when(upper != 0)
            def _():
                def body(l, carry):
                    for j in range(2):
                        for r in range(rows):
                            span = slice(r * COLS, (r + 1) * COLS)
                            some = near[j, pl.ds(l, depth), :, span].reshape(depth * block, COLS)
                            mixed = rounded(jnp.dot(coef[half + l], some, preferred_element_type=F32))
                            here = pl.ds(pl.multiple_of(l * block, block), block)
                            add(j, half + l, span, jnp.exp2(table_ref[j, here, span] + mixed))
                    return carry

                lax.fori_loop(lead, half, body, 0)

            for j in range(2):
                tile = tile_of(me, lines, j)

                @pl.when(jnp.logical_not(at_ends) & (tile >= low + first) & (tile < low + half))
                def _():
                    if at_ends:
                        return
                    best, rest = pick(cand_ref, j, tile * block, pw.at[j], 0, block)
                    best_out[j : j + 1] = best
                    acc[j] += rest

                sums[j : j + 1] = jnp.sum(acc[j], axis=0, keepdims=True)

    flops = (half * 2 + lead) * 2 * block * depth * block * pixels
    scratch = [
        ((2, lead + half, block, pixels), BF16),
        ((n, block, wide), BF16),
        ((tall, tall), BF16),
        ((depth * block, (depth + lead) * block), BF16),
        ((2, block, pixels), F32),
        ((2, 8, pixels), F32),
    ]
    outs = [((2, pixels), F32)]
    if not at_ends:
        outs += [((2, pixels), F32), ((2, tall, pixels), F32), ((tall, tall), BF16)]
    given = (table, *pieces, *held, *partner)
    return pl.pallas_call(
        kernel,
        in_specs=[SMEM] + [VMEM] * len(given),
        out_specs=[VMEM] * len(outs),
        out_shape=[jax.ShapeDtypeStruct(*out) for out in outs],
        scratch_shapes=[pltpu.VMEM(*one) for one in scratch],
        compiler_params=grant(*scratch, *outs, *[(x.shape, x.dtype) for x in given]),
        cost_estimate=pl.CostEstimate(flops=flops, bytes_accessed=8 << 20, transcendentals=0),
        name="stage_one",
    )(cand, *given)


def stage_two(cand, one, median, other, middle, outer, half, depth, bands):
    block, pixels = one[2].shape[1] // (depth - 1), one[2].shape[2]
    lead, lines = depth - 1, half // 2
    rows = pixels // COLS
    tall = lead * block
    nm, no = len(middle), len(outer)

    def kernel(cand_ref, sums, best_one, partial, coef, median, other_ref, *refs):
        middle_refs, refs = refs[:nm], refs[nm:]
        outer_refs, refs = refs[: 2 * no], refs[2 * no :]
        outs, (far, pw, acc, best) = refs[:2], refs[2:]
        me, _ = places()
        upper = me // half
        level = me // lines

        @pl.when((level == 1) | (level == 2))
        def _():
            base = jnp.where(upper == 0, half, half - lead)

            def put(j, row, unit):
                place = row - base
                far[j, jnp.where((place >= 0) & (place < lead), place, lead)] = unit

            for j in range(2):
                for (k, _), ref in zip(middle, middle_refs):
                    put(j, me ^ 3 * lines ^ k, ref[j])
                for i, (low, high, _) in enumerate(outer):
                    put(j, jnp.where(upper == 0, 3 * lines + high, low), outer_refs[2 * i + j][...])
                best[...] = best_one[j : j + 1]
                tile = tile_of(me, lines, j)
                for r in range(rows):
                    span = slice(r * COLS, (r + 1) * COLS)
                    some = far[j, :lead, :, span].reshape(tall, COLS)
                    mixed = jnp.dot(coef[...], some, preferred_element_type=F32) + partial[j, :, span]
                    power = jnp.exp2(median[j, :, span] + rounded(mixed))
                    total = jnp.zeros((8, COLS), F32)
                    for l in range(lead):
                        total += jnp.where(tile == half + l, 0.0, fold(power[l * block : (l + 1) * block]))
                    acc[:, span] = total

                    @pl.when(upper != 0)
                    def _():
                        pw[:, span] = power

                @pl.when((tile >= half) & (tile < half + lead))
                def _():
                    top = pl.multiple_of((tile - half) * block, block)
                    first, rest = pick(cand_ref, j, tile * block, pw, top, block)
                    best[...] = first
                    acc[...] += rest

                total = sums[j : j + 1] + other_ref[j : j + 1] + jnp.sum(acc[...], axis=0, keepdims=True)
                scale = 1.0 / math.log(10.0)
                sinr = jnp.log(best[...] / total) * scale
                share = jnp.sum(sinr, axis=1, keepdims=True) / float(pixels * bands)
                outs[j][0:1] = jnp.log(best[...]) * scale
                outs[j][1:2] = sinr
                outs[j][2:3] = jnp.broadcast_to(share, (1, pixels))

    scratch = [((2, lead + 1, block, pixels), BF16), ((tall, pixels), F32), ((8, pixels), F32), ((1, pixels), F32)]
    given = [x for _, x in middle] + [x for _, _, pair in outer for x in pair]
    held = [(x.shape, x.dtype) for x in (*one[2:], median, *given)]
    return pl.pallas_call(
        kernel,
        in_specs=[SMEM] + [VMEM] * (6 + len(given)),
        out_specs=[VMEM] * 2,
        out_shape=[jax.ShapeDtypeStruct((3, pixels), F32)] * 2,
        scratch_shapes=[pltpu.VMEM(*shape) for shape in scratch],
        compiler_params=grant(*scratch, *held),
        name="stage_two",
    )(cand, *one, median, other, *given)


def plan_of(n, lead):
    half, lines = n // 2, n // 4
    cross = range(half - lead, half + lead)
    row = lambda s, k: s // lines * lines + (s % lines ^ k)
    middle = {k: [s for s in range(n) if s // lines in (1, 2) and row(s, k) in cross] for k in range(lines)}
    low = [r for r in range(lines) if r in cross]
    high = [r for r in range(lines) if 3 * lines + r in cross]
    assert len(low) == len(high)
    return middle, list(zip(low, high))


def shards(fields, factor, pattern, tx_power, site_position, candidates):
    _, tiles, pixels = fields.shape
    depth = factor.shape[1]
    n, bands = lax.axis_size("site"), lax.axis_size("band")
    half, lines, lead = n // 2, n // 4, depth - 1
    assert tiles == n and half >= lead
    height = tiles // 8
    middle, outer = plan_of(n, lead)
    me = lax.axis_index("site")
    level = me // lines

    def swap(x, k, axis="site", sources=None):
        count = n if axis == "site" else bands
        sources = range(count) if sources is None else sources
        return lax.ppermute(x, axis, [(s, s ^ k) for s in sources])

    class0, class1, own_part = split_tiles(fields, factor, pattern, lines)

    ends = [s for s in range(n) if s // lines in (0, 3)]
    pass_on = {0: class1[0]}
    pass_on.update({k: swap(class1[k], k) for k in range(1, lines)})
    held = {0: class0[0]}
    held.update({k: [swap(class0[k][j], k) for j in range(2)] for k in range(1, lines)})
    far = [(k, swap(pass_on[k], 3 * lines, sources=middle[k])) for k in range(lines) if middle[k]]
    partner = [swap(pass_on[k], lines) for k in range(lines)]
    ends_far = []
    for low, high in outer:
        at = (me % lines) ^ jnp.where(level == 0, low, high)
        pair = []
        for j in range(2):
            here, _ = lax.optimization_barrier((at, jnp.int32(j)))
            unit = held[0][j]
            for k in range(1, lines):
                unit = jnp.where(here == k, held[k][j], unit)
            pair.append(swap(unit, 2 * lines, sources=ends))
        ends_far.append((low, high, pair))

    line_part = jnp.stack([own_part] + [swap(own_part, k) for k in range(1, lines)])
    next_part = swap(line_part, lines)
    middle_part = swap(line_part, 3 * lines, sources=range(2 * lines, 3 * lines))
    ends_part = []
    for low, high in outer:
        at = (me % lines) ^ high
        row = line_part[0]
        for k in range(1, lines):
            row = jnp.where(at == k, line_part[k], row)
        ends_part.append(swap(row, 2 * lines, sources=range(3 * lines, n)))
    groups = [line_part, next_part, middle_part] + [jnp.broadcast_to(x[None], line_part.shape) for x in ends_part]
    mine = jnp.stack(groups)
    pieces = [mine, swap(mine, 1, axis="band")]

    near_cand = swap(candidates, lines)
    cand = jnp.concatenate([near_cand, candidates])
    tx = tx_power.reshape(1, -1)
    table, *here = reach_tables(tx, site_position, held[0], half, depth, pixels, height)
    median = middle_tables(tx, site_position, half, depth, pixels, height)
    units = here + [x for k in range(1, lines) for x in held[k]]
    stage = functools.partial(
        stage_one,
        table=table,
        pieces=pieces,
        ends_rows=[high for _, high in outer],
        held=units,
        partner=partner,
        half=half,
        depth=depth,
    )
    (ends_sums,) = stage(True, cand)
    other = swap(ends_sums, 2 * lines, sources=ends)
    one = stage(False, cand)
    inner = [s for s in range(n) if s // lines in (1, 2)]
    moving, own = stage_two(cand, one, median, other, far, ends_far, half, depth, bands)
    moved = swap(moving, lines, sources=inner)
    done = jnp.where((level == 1) | (level == 2), own, moved)
    share = done[2:3, :128]
    bit = 1
    while bit < bands:
        share = share + swap(share, bit, axis="band")
        bit *= 2
    return done[0:1], done[1:2], share[0, :1]


def solution(mesh):
    placed = (
        P("site", None, "band"),
        P("site", None, None),
        P("site", None),
        P(),
        P(),
        P("site", None),
    )

    return jax.shard_map(
        shards,
        mesh=mesh,
        in_specs=placed,
        out_specs=(P("site", "band"), P("site", "band"), P("site")),
        check_vma=False,
    )
```

time: 100 us -> 87.6 us (0.88)
  starting transfers between devices: 50 us -> 31.9 us
  waiting for transfers between devices: 29.9 us -> 44.6 us
  Pallas kernels: 12.4 us -> 7.23 us
  local copies, waits for them, and re-layouts: 4.69 us -> 2 us
    ppermute x19, starting transfers between devices: 50 us -> 31.9 us  [swap(): return lax.ppermute(x, axis, [(s, s ^ k) for s in sources])]
    ppermute x19, waiting for transfers between devices: 29.9 us -> 44.6 us  [swap(): return lax.ppermute(x, axis, [(s, s ^ k) for s in sources])]
    unnamed x16 -> x6, local copies, waits for them, and re-layouts: 4.69 us -> 1.39 us
    pallas_call x4, Pallas kernels: 7.08 us -> 4.29 us  [the longest x1 2.36 us: split_tiles(): pl.pallas_call(kernel, in_specs=[HBM] * 3, out_specs=[VMEM] * (3 * lines...]
    pallas_call x1 -> x2, Pallas kernels: 5.36 us -> 2.93 us  [stage_one(): pl.pallas_call(kernel, in_specs=[SMEM] + [VMEM] * len(given), out_specs=[...]
  transfers between devices with their start and end apart: 19 -> 19, of which waited for: 6 -> 9; matrix products, arithmetic and copies ran while one was open for 0% -> 1% of each run, Pallas kernels for 7% -> 5%
where the time goes in v1:
time: 87.6 us; the launch traced here: 87.2 us
  waiting for transfers between devices  44.6 us (51%)
  starting transfers between devices  31.9 us (36%)
  Pallas kernels  7.23 us (8%)
  local copies, waits for them, and re-layouts  2 us (2%)
    ppermute x19, waiting for transfers between devices, swap(): return lax.ppermute(x, axis, [(s, s ^ k) for s in sources])  44.6 us
    ppermute x19, starting transfers between devices, swap(): return lax.ppermute(x, axis, [(s, s ^ k) for s in sources])  31.9 us
    pallas_call x2, Pallas kernels, stage_one(): pl.pallas_call(kernel, in_specs=[SMEM] + [VMEM] * len(given), out_specs=[...  2.93 us
    pallas_call x1, Pallas kernels, split_tiles(): pl.pallas_call(kernel, in_specs=[HBM] * 3, out_specs=[VMEM] * (3 * lines...  2.36 us
  transfers between devices with their start and end apart: 19, of which 9 were waited for; matrix products, arithmetic and copies ran while one was open for 1% of the time, Pallas kernels for 5%

profile of v1, /device:TPU:0, one launch (start us, length us, event | category | flops | bytes accessed | tf_op | source)
XLA Modules:
  0.0 87.2 jit_solution(4581439642129904905)
XLA Ops:
  0.6 0.0 copy-start.2
  0.6 2.4 %split_tiles.1 = (bf16[128,1024]{1,0:T(8,128)(2,1)S(1)}, bf16[128,1024]{1,0:T(8,128)(2,1)S(1)}, bf16[128,1024]{1,0:T(8,128)(2,1)S(1)}, bf16[128,1024]{1,0:T(8,12...) custom-call(s32[1,3]{1,0:T(1,128)} %pattern_ref.1, ...), custom_call_target="tpu_custom_call" | custom-call | tf_op jit(solution)/shard_map/split_tiles/pallas_call | solution.py:87
  3.0 3.0 %collective-permute-start.1 = (bf16[64,512]{1,0:T(8,128)(2,1)S(1)}, bf16[64,512]{1,0:T(8,128)(2,1)S(1)}, u32[]{:S(2)}, u32[]{:S(2)}) collective-permute-start(bf16[64,512]{1,0:T(8,128)(2,1)S(1)} %get-tuple-element.24), channel_id=1, source_target_pairs={{0,4},{4,0},{8,12},{12,8},{16,20},{20,16},{24,28},{28,24},{1,5},{5... | collective-permute-start | bytes 196616 | tf_op jit(solution)/shard_map/ppermute | solution.py:479
  6.0 0.1 collective-permute-start.9
  6.1 2.4 %collective-permute-done.1 = bf16[64,512]{1,0:T(8,128)(2,1)S(1)} collective-permute-done((bf16[64,512]{1,0:T(8,128)(2,1)S(1)}, bf16[64,512]{1,0:T(8,128)(2,1)S(1)}, u32[]{:S(2)}, u32[]{:S(2)}) %collective-permute-start.1) | collective-permute-done | bytes 65568 | tf_op jit(solution)/shard_map/ppermute | solution.py:479
  8.5 2.6 %collective-permute-start.2 = (bf16[2,64,512]{2,1,0:T(8,128)(2,1)S(1)}, bf16[2,64,512]{2,1,0:T(8,128)(2,1)S(1)}, u32[]{:S(2)}, u32[]{:S(2)}) collective-permute-start(bf16[2,64,512]{2,1,0:T(8,128)(2,1)S(1)} %get-tuple-element.40), channel_id=1, source_target_pairs={{0,8},{4,12},{8,0},{12,4},{16,24},{20,28},{24,16},{28,20},{1,9},{5... | collective-permute-start | bytes 393224 | tf_op jit(solution)/shard_map/ppermute | solution.py:479
  11.1 0.7 collective-permute-start.3
  11.8 0.7 collective-permute-start.4
  12.5 1.6 %collective-permute-start.6 = (bf16[128,1024]{1,0:T(8,128)(2,1)S(1)}, bf16[128,1024]{1,0:T(8,128)(2,1)S(1)}, u32[]{:S(2)}, u32[]{:S(2)}) collective-permute-start(bf16[128,1024]{1,0:T(8,128)(2,1)S(1)} %get-tuple-element.27), channel_id=1, source_target_pairs={{0,4},{4,0},{8,12},{12,8},{16,20},{20,16},{24,28},{28,24},{1,5},{5... | collective-permute-start | bytes 786440 | tf_op jit(solution)/shard_map/ppermute | solution.py:479
  14.1 0.0 collective-permute-done.4
  14.1 0.5 collective-permute-start.7
  14.6 0.0 copy-start
  14.6 0.7 copy-done
  15.2 0.0 copy-start.1
  15.2 0.7 copy-done.1
  15.9 1.4 %reach_tables.1 = (f32[2,512,1024]{2,1,0:T(8,128)S(1)}, bf16[128,1024]{1,0:T(8,128)(2,1)S(1)}, bf16[128,1024]{1,0:T(8,128)(2,1)S(1)}) custom-call(f32[1,1024]{1,0:T(1,128)S(1)} %bitcast.11, f32[2,1024]{1,0:T(2,128)S(1)} %copy-done, bf16[128,1024]{1,0:T(8,128)(2,1)S(1)} %get-tuple-element.21.unit0, bf16[128,1024]{1,0:T(8,128)(2,1)S(1)} %get-tuple-element.22.unit1), custom_call_target="tpu_custom_call" | custom-call | flops 20971520 | bytes 8388608 | tf_op jit(solution)/shard_map/reach_tables/pallas_call | solution.py:191
  17.3 0.0 collective-permute-done.2
  17.3 8.0 %collective-permute-start.8 = (bf16[2,128,1024]{2,1,0:T(8,128)(2,1)S(1)}, bf16[2,128,1024]{2,1,0:T(8,128)(2,1)S(1)}, u32[]{:S(2)}, u32[]{:S(2)}) collective-permute-start(bf16[2,128,1024]{2,1,0:T(8,128)(2,1)S(1)} %get-tuple-element.29), channel_id=1, source_target_pairs={{0,8},{4,12},{8,0},{12,4},{16,24},{20,28},{24,16},{28,20},{1,9},{5... | collective-permute-start | bytes 1572872 | tf_op jit(solution)/shard_map/ppermute | solution.py:479
  25.3 0.0 collective-permute-done.3
  25.3 0.0 copy-done.2
  25.3 0.1 collective-permute-start
  25.4 0.1 pad_maximum_fusion.refs_0_
  25.5 9.0 %collective-permute-done = s32[1,16]{1,0:T(1,128)S(1)} collective-permute-done((s32[1,16]{1,0:T(1,128)S(1)}, s32[1,16]{1,0:T(1,128)S(1)}, u32[]{:S(2)}, u32[]{:S(2)}) %collective-permute-start) | collective-permute-done | bytes 96 | tf_op jit(solution)/shard_map/ppermute | solution.py:479
  34.5 0.0 collective-permute-start.5
  34.5 0.0 collective-permute-done.9
  34.5 1.7 %collective-permute-start.10 = (bf16[2,128,1024]{2,1,0:T(8,128)(2,1)}, bf16[2,128,1024]{2,1,0:T(8,128)(2,1)S(1)}, u32[]{:S(2)}, u32[]{:S(2)}) collective-permute-start(bf16[2,128,1024]{2,1,0:T(8,128)(2,1)} %collective-permute-done.9), channel_id=1, source_target_pairs={{0,8},{4,12},{8,0},{12,4},{16,24},{20,28},{24,16},{28,20},{1,9},{5... | collective-permute-start | bytes 1572872 | tf_op jit(solution)/shard_map/ppermute | solution.py:479
  36.2 0.0 collective-permute-done.6.refs_4_
  36.2 0.7 collective-permute-start.12
  36.9 0.0 collective-permute-done.7.refs_5_
  37.0 0.7 collective-permute-start.13
  37.7 0.0 collective-permute-done.8.refs_6_
  37.7 6.1 %collective-permute-start.14 = (bf16[128,1024]{1,0:T(8,128)(2,1)S(1)}, bf16[128,1024]{1,0:T(8,128)(2,1)S(1)}, u32[]{:S(2)}, u32[]{:S(2)}) collective-permute-start(bf16[128,1024]{1,0:T(8,128)(2,1)S(1)} %broadcast_select_fusion.1), channel_id=1, source_target_pairs={{0,16},{4,20},{24,8},{28,12},{1,17},{5,21},{25,9},{29,13},{2,18},{... | collective-permute-start | bytes 786440 | tf_op jit(solution)/shard_map/ppermute | solution.py:479
  43.9 0.0 collective-permute-done.5.refs_1_
  43.9 1.3 %collective-permute-start.15 = (bf16[128,1024]{1,0:T(8,128)(2,1)S(1)}, bf16[128,1024]{1,0:T(8,128)(2,1)S(1)}, u32[]{:S(2)}, u32[]{:S(2)}) collective-permute-start(bf16[128,1024]{1,0:T(8,128)(2,1)S(1)} %broadcast_select_fusion), channel_id=1, source_target_pairs={{0,16},{4,20},{24,8},{28,12},{1,17},{5,21},{25,9},{29,13},{2,18},{... | collective-permute-start | bytes 786440 | tf_op jit(solution)/shard_map/ppermute | solution.py:479
  45.2 3.9 %collective-permute-done.10.refs_7_ = bf16[2,128,1024]{2,1,0:T(8,128)(2,1)S(1)} collective-permute-done((bf16[2,128,1024]{2,1,0:T(8,128)(2,1)}, bf16[2,128,1024]{2,1,0:T(8,128)(2,1)S(1)}, u32[]{:S(2)}, u32[]{:S(2)}) %collective-permute-start.10) | collective-permute-done | bytes 524320 | tf_op jit(solution)/shard_map/ppermute | solution.py:479
  49.0 2.4 %stage_one.3 = f32[2,1024]{1,0:T(2,128)S(1)} custom-call(s32[2,16]{1,0:T(2,128)S(1)} %pad_add_fusion.cand_ref, f32[2,512,1024]{2,1,0:T(8,128)S(1)} %get-tuple-element.23.table_ref, bf16[4,2,64,512]{3,2,1,0:T(8,128)(2,1)S(1)} %pad_maximum_fusion.refs_0_, bf16[4,2,64,512]{3,2,1,0:T(8,128)(2,1)S(1)} %collective-permute-done.5.refs_1_, ...), custom_call_target="tpu_custom_call" | custom-call | flops 1476395008 | bytes 8388608 | tf_op jit(solution)/shard_map/stage_one/pallas_call | solution.py:369
  51.4 1.3 %collective-permute-start.11 = (f32[2,1024]{1,0:T(2,128)S(1)}, f32[2,1024]{1,0:T(2,128)S(1)}, u32[]{:S(2)}, u32[]{:S(2)}) collective-permute-start(f32[2,1024]{1,0:T(2,128)S(1)} %stage_one.3), channel_id=1, source_target_pairs={{0,16},{4,20},{24,8},{28,12},{1,17},{5,21},{25,9},{29,13},{2,18},{... | collective-permute-start | bytes 24584 | tf_op jit(solution)/shard_map/ppermute | solution.py:479
  52.7 0.6 stage_one.2
  53.3 1.1 %collective-permute-done.14.refs_2_ = bf16[128,1024]{1,0:T(8,128)(2,1)S(1)} collective-permute-done((bf16[128,1024]{1,0:T(8,128)(2,1)S(1)}, bf16[128,1024]{1,0:T(8,128)(2,1)S(1)}, u32[]{:S(2)}, u32[]{:S(2)}) %collective-permute-start.14) | collective-permute-done | bytes 262176 | tf_op jit(solution)/shard_map/ppermute | solution.py:479
  54.4 5.2 %collective-permute-done.15.refs_3_ = bf16[128,1024]{1,0:T(8,128)(2,1)S(1)} collective-permute-done((bf16[128,1024]{1,0:T(8,128)(2,1)S(1)}, bf16[128,1024]{1,0:T(8,128)(2,1)S(1)}, u32[]{:S(2)}, u32[]{:S(2)}) %collective-permute-start.15) | collective-permute-done | bytes 262176 | tf_op jit(solution)/shard_map/ppermute | solution.py:479
  59.7 0.0 collective-permute-done.12.refs_0_
  59.7 0.0 collective-permute-done.13.refs_1_
  59.7 0.1 collective-permute-done.11.other_ref
  59.8 0.6 stage_two.1
  60.3 1.3 %collective-permute-start.16 = (f32[3,1024]{1,0:T(4,128)S(1)}, f32[3,1024]{1,0:T(4,128)S(1)}, u32[]{:S(2)}, u32[]{:S(2)}) collective-permute-start(f32[3,1024]{1,0:T(4,128)S(1)} %get-tuple-element.38), channel_id=1, source_target_pairs={{8,0},{12,4},{16,24},{20,28},{9,1},{13,5},{17,25},{21,29},{10,2},{... | collective-permute-start | bytes 36872 | tf_op jit(solution)/shard_map/ppermute | solution.py:479
  61.6 20.3 %collective-permute-done.16 = f32[3,1024]{1,0:T(4,128)S(1)} collective-permute-done((f32[3,1024]{1,0:T(4,128)S(1)}, f32[3,1024]{1,0:T(4,128)S(1)}, u32[]{:S(2)}, u32[]{:S(2)}) %collective-permute-start.16) | collective-permute-done | bytes 12320 | tf_op jit(solution)/shard_map/ppermute | solution.py:479
  81.9 0.1 collective-permute-start.17
  82.0 1.1 %collective-permute-done.17 = f32[1,128]{1,0:T(1,128)S(1)} collective-permute-done((f32[1,128]{1,0:T(1,128)S(1)}, f32[1,128]{1,0:T(1,128)S(1)}, u32[]{:S(2)}, u32[]{:S(2)}) %collective-permute-start.17) | collective-permute-done | bytes 544 | tf_op jit(solution)/shard_map/ppermute | solution.py:479
  83.2 1.5 %collective-permute-start.18 = (f32[1,128]{1,0:T(1,128)S(1)}, f32[1,128]{1,0:T(1,128)S(1)}, u32[]{:S(2)}, u32[]{:S(2)}) collective-permute-start(f32[1,128]{1,0:T(1,128)S(1)} %slice_add_fusion), channel_id=1, source_target_pairs={{0,2},{1,3},{2,0},{3,1},{4,6},{5,7},{6,4},{7,5},{8,10},{9,11},{10,... | collective-permute-start | bytes 1544 | tf_op jit(solution)/shard_map/ppermute | solution.py:479
  84.7 0.6 fusion.1
  85.3 1.4 %collective-permute-done.18 = f32[1,128]{1,0:T(1,128)S(1)} collective-permute-done((f32[1,128]{1,0:T(1,128)S(1)}, f32[1,128]{1,0:T(1,128)S(1)}, u32[]{:S(2)}, u32[]{:S(2)}) %collective-permute-start.18) | collective-permute-done | bytes 544 | tf_op jit(solution)/shard_map/ppermute | solution.py:479
  86.7 0.5 add.14
  (10 shorter events, 0.1 us)
Async XLA Ops:
  0.6 24.7 %copy-start.2 = (s32[1,16]{1,0:T(1,128)S(1)}, s32[1,16]{1,0:T(1,128)}, u32[]{:S(2)}) copy-start(s32[1,16]{1,0:T(1,128)} %param.11) | copy-start | bytes 196
  3.0 5.5 %collective-permute-start.1 = (bf16[64,512]{1,0:T(8,128)(2,1)S(1)}, bf16[64,512]{1,0:T(8,128)(2,1)S(1)}, u32[]{:S(2)}, u32[]{:S(2)}) collective-permute-start(bf16[64,512]{1,0:T(8,128)(2,1)S(1)} %get-tuple-element.24), channel_id=1, source_target_pairs={{0,4},{4,0},{8,12},{12,8},{16,20},{20,16},{24,28},{28,24},{1,5},{5... | collective-permute-start | bytes 196616 | tf_op jit(solution)/shard_map/ppermute | solution.py:479
  6.0 28.4 %collective-permute-start.9 = (bf16[2,128,1024]{2,1,0:T(8,128)(2,1)S(1)}, bf16[2,128,1024]{2,1,0:T(8,128)(2,1)}, u32[]{:S(2)}, u32[]{:S(2)}) collective-permute-start(bf16[2,128,1024]{2,1,0:T(8,128)(2,1)S(1)} %get-tuple-element.30), channel_id=1, source_target_pairs={{0,4},{4,0},{8,12},{12,8},{16,20},{20,16},{24,28},{28,24},{1,5},{5... | collective-permute-start | bytes 1572872 | tf_op jit(solution)/shard_map/ppermute | solution.py:479
  8.5 8.8 %collective-permute-start.2 = (bf16[2,64,512]{2,1,0:T(8,128)(2,1)S(1)}, bf16[2,64,512]{2,1,0:T(8,128)(2,1)S(1)}, u32[]{:S(2)}, u32[]{:S(2)}) collective-permute-start(bf16[2,64,512]{2,1,0:T(8,128)(2,1)S(1)} %get-tuple-element.40), channel_id=1, source_target_pairs={{0,8},{4,12},{8,0},{12,4},{16,24},{20,28},{24,16},{28,20},{1,9},{5... | collective-permute-start | bytes 393224 | tf_op jit(solution)/shard_map/ppermute | solution.py:479
  11.1 14.2 %collective-permute-start.3 = (bf16[2,64,512]{2,1,0:T(8,128)(2,1)S(1)}, bf16[2,64,512]{2,1,0:T(8,128)(2,1)S(1)}, u32[]{:S(2)}, u32[]{:S(2)}) collective-permute-start(bf16[2,64,512]{2,1,0:T(8,128)(2,1)S(1)} %get-tuple-element.40), channel_id=1, source_target_pairs={{16,8},{20,12},{17,9},{21,13},{18,10},{22,14},{19,11},{23,15}} | collective-permute-start | bytes 393224 | tf_op jit(solution)/shard_map/ppermute | solution.py:479
  11.8 2.3 %collective-permute-start.4 = (bf16[64,512]{1,0:T(8,128)(2,1)S(1)}, bf16[64,512]{1,0:T(8,128)(2,1)S(1)}, u32[]{:S(2)}, u32[]{:S(2)}) collective-permute-start(bf16[64,512]{1,0:T(8,128)(2,1)S(1)} %broadcast_select_fusion.2), channel_id=1, source_target_pairs={{24,8},{28,12},{25,9},{29,13},{26,10},{30,14},{27,11},{31,15}} | collective-permute-start | bytes 196616 | tf_op jit(solution)/shard_map/ppermute | solution.py:479
  12.5 23.8 %collective-permute-start.6 = (bf16[128,1024]{1,0:T(8,128)(2,1)S(1)}, bf16[128,1024]{1,0:T(8,128)(2,1)S(1)}, u32[]{:S(2)}, u32[]{:S(2)}) collective-permute-start(bf16[128,1024]{1,0:T(8,128)(2,1)S(1)} %get-tuple-element.27), channel_id=1, source_target_pairs={{0,4},{4,0},{8,12},{12,8},{16,20},{20,16},{24,28},{28,24},{1,5},{5... | collective-permute-start | bytes 786440 | tf_op jit(solution)/shard_map/ppermute | solution.py:479
  14.1 22.9 %collective-permute-start.7 = (bf16[128,1024]{1,0:T(8,128)(2,1)S(1)}, bf16[128,1024]{1,0:T(8,128)(2,1)S(1)}, u32[]{:S(2)}, u32[]{:S(2)}) collective-permute-start(bf16[128,1024]{1,0:T(8,128)(2,1)S(1)} %get-tuple-element.28), channel_id=1, source_target_pairs={{0,4},{4,0},{8,12},{12,8},{16,20},{20,16},{24,28},{28,24},{1,5},{5... | collective-permute-start | bytes 786440 | tf_op jit(solution)/shard_map/ppermute | solution.py:479
  14.6 0.7 copy-start
  15.2 0.7 copy-start.1
  17.3 20.4 %collective-permute-start.8 = (bf16[2,128,1024]{2,1,0:T(8,128)(2,1)S(1)}, bf16[2,128,1024]{2,1,0:T(8,128)(2,1)S(1)}, u32[]{:S(2)}, u32[]{:S(2)}) collective-permute-start(bf16[2,128,1024]{2,1,0:T(8,128)(2,1)S(1)} %get-tuple-element.29), channel_id=1, source_target_pairs={{0,8},{4,12},{8,0},{12,4},{16,24},{20,28},{24,16},{28,20},{1,9},{5... | collective-permute-start | bytes 1572872 | tf_op jit(solution)/shard_map/ppermute | solution.py:479
  25.3 9.2 %collective-permute-start = (s32[1,16]{1,0:T(1,128)S(1)}, s32[1,16]{1,0:T(1,128)S(1)}, u32[]{:S(2)}, u32[]{:S(2)}) collective-permute-start(s32[1,16]{1,0:T(1,128)S(1)} %copy-done.2), channel_id=1, source_target_pairs={{0,8},{4,12},{8,0},{12,4},{16,24},{20,28},{24,16},{28,20},{1,9},{5... | collective-permute-start | bytes 200 | tf_op jit(solution)/shard_map/ppermute | solution.py:479
  34.5 9.4 %collective-permute-start.5 = (bf16[4,2,64,512]{3,2,1,0:T(8,128)(2,1)S(1)}, bf16[4,2,64,512]{3,2,1,0:T(8,128)(2,1)S(1)}, u32[]{:S(2)}, u32[]{:S(2)}) collective-permute-start(bf16[4,2,64,512]{3,2,1,0:T(8,128)(2,1)S(1)} %pad_maximum_fusion.refs_0_), channel_id=1, source_target_pairs={{0,1},{1,0},{2,3},{3,2},{4,5},{5,4},{6,7},{7,6},{8,9},{9,8},{10,11... | collective-permute-start | bytes 1572872 | tf_op jit(solution)/shard_map/ppermute | solution.py:479
  34.5 14.5 %collective-permute-start.10 = (bf16[2,128,1024]{2,1,0:T(8,128)(2,1)}, bf16[2,128,1024]{2,1,0:T(8,128)(2,1)S(1)}, u32[]{:S(2)}, u32[]{:S(2)}) collective-permute-start(bf16[2,128,1024]{2,1,0:T(8,128)(2,1)} %collective-permute-done.9), channel_id=1, source_target_pairs={{0,8},{4,12},{8,0},{12,4},{16,24},{20,28},{24,16},{28,20},{1,9},{5... | collective-permute-start | bytes 1572872 | tf_op jit(solution)/shard_map/ppermute | solution.py:479
  36.2 23.4 %collective-permute-start.12 = (bf16[2,128,1024]{2,1,0:T(8,128)(2,1)S(1)}, bf16[2,128,1024]{2,1,0:T(8,128)(2,1)S(1)}, u32[]{:S(2)}, u32[]{:S(2)}) collective-permute-start(bf16[2,128,1024]{2,1,0:T(8,128)(2,1)S(1)} %get-tuple-element.29), channel_id=1, source_target_pairs={{8,16},{12,20},{16,8},{20,12},{9,17},{13,21},{17,9},{21,13},{10,18... | collective-permute-start | bytes 1572872 | tf_op jit(solution)/shard_map/ppermute | solution.py:479
  37.0 22.7 %collective-permute-start.13 = (bf16[2,128,1024]{2,1,0:T(8,128)(2,1)}, bf16[2,128,1024]{2,1,0:T(8,128)(2,1)S(1)}, u32[]{:S(2)}, u32[]{:S(2)}) collective-permute-start(bf16[2,128,1024]{2,1,0:T(8,128)(2,1)} %collective-permute-done.9), channel_id=1, source_target_pairs={{8,16},{12,20},{16,8},{20,12},{9,17},{13,21},{17,9},{21,13},{10,18... | collective-permute-start | bytes 1572872 | tf_op jit(solution)/shard_map/ppermute | solution.py:479
  37.7 16.7 %collective-permute-start.14 = (bf16[128,1024]{1,0:T(8,128)(2,1)S(1)}, bf16[128,1024]{1,0:T(8,128)(2,1)S(1)}, u32[]{:S(2)}, u32[]{:S(2)}) collective-permute-start(bf16[128,1024]{1,0:T(8,128)(2,1)S(1)} %broadcast_select_fusion.1), channel_id=1, source_target_pairs={{0,16},{4,20},{24,8},{28,12},{1,17},{5,21},{25,9},{29,13},{2,18},{... | collective-permute-start | bytes 786440 | tf_op jit(solution)/shard_map/ppermute | solution.py:479
  43.9 15.8 %collective-permute-start.15 = (bf16[128,1024]{1,0:T(8,128)(2,1)S(1)}, bf16[128,1024]{1,0:T(8,128)(2,1)S(1)}, u32[]{:S(2)}, u32[]{:S(2)}) collective-permute-start(bf16[128,1024]{1,0:T(8,128)(2,1)S(1)} %broadcast_select_fusion), channel_id=1, source_target_pairs={{0,16},{4,20},{24,8},{28,12},{1,17},{5,21},{25,9},{29,13},{2,18},{... | collective-permute-start | bytes 786440 | tf_op jit(solution)/shard_map/ppermute | solution.py:479
  51.4 8.4 %collective-permute-start.11 = (f32[2,1024]{1,0:T(2,128)S(1)}, f32[2,1024]{1,0:T(2,128)S(1)}, u32[]{:S(2)}, u32[]{:S(2)}) collective-permute-start(f32[2,1024]{1,0:T(2,128)S(1)} %stage_one.3), channel_id=1, source_target_pairs={{0,16},{4,20},{24,8},{28,12},{1,17},{5,21},{25,9},{29,13},{2,18},{... | collective-permute-start | bytes 24584 | tf_op jit(solution)/shard_map/ppermute | solution.py:479
  60.3 21.6 %collective-permute-start.16 = (f32[3,1024]{1,0:T(4,128)S(1)}, f32[3,1024]{1,0:T(4,128)S(1)}, u32[]{:S(2)}, u32[]{:S(2)}) collective-permute-start(f32[3,1024]{1,0:T(4,128)S(1)} %get-tuple-element.38), channel_id=1, source_target_pairs={{8,0},{12,4},{16,24},{20,28},{9,1},{13,5},{17,25},{21,29},{10,2},{... | collective-permute-start | bytes 36872 | tf_op jit(solution)/shard_map/ppermute | solution.py:479
  81.9 1.2 %collective-permute-start.17 = (f32[1,128]{1,0:T(1,128)S(1)}, f32[1,128]{1,0:T(1,128)S(1)}, u32[]{:S(2)}, u32[]{:S(2)}) collective-permute-start(f32[1,128]{1,0:T(1,128)S(1)} %slice.18), channel_id=1, source_target_pairs={{0,1},{1,0},{2,3},{3,2},{4,5},{5,4},{6,7},{7,6},{8,9},{9,8},{10,11... | collective-permute-start | bytes 1544 | tf_op jit(solution)/shard_map/ppermute | solution.py:479
  83.2 3.6 %collective-permute-start.18 = (f32[1,128]{1,0:T(1,128)S(1)}, f32[1,128]{1,0:T(1,128)S(1)}, u32[]{:S(2)}, u32[]{:S(2)}) collective-permute-start(f32[1,128]{1,0:T(1,128)S(1)} %slice_add_fusion), channel_id=1, source_target_pairs={{0,2},{1,3},{2,0},{3,1},{4,6},{5,7},{6,4},{7,5},{8,10},{9,11},{10,... | collective-permute-start | bytes 1544 | tf_op jit(solution)/shard_map/ppermute | solution.py:479
